TPU v7x, 32 devices: a whole 2x2x4 slice. The times are simulated.
32 devices in a mesh: slab: 2 (over x), row: 8 (over z, y), col: 2 (over core).
Axes of the slice: x: 2, y: 2, z: 4, core: 2. Of those that a mesh axis runs over, the one named last changes fastest.
Arguments:
- points: bfloat16 [9, 32, 131072], P(None, None, ('slab', 'row', 'col')), parts along dimension 2, may hold values from -6 to 6
- pillar_cell: int32 [131072], P(('slab', 'row', 'col')), parts along dimension 0, may hold values from 0 to 65535, as said below
- point_count: int32 [131072], P(('slab', 'row', 'col')), parts along dimension 0, may hold values from 1 to 32
- tile_count: int32 [512], P(('slab', 'row', 'col')), parts along dimension 0, may hold values from 0 to 256, as said below
- point_embed: bfloat16 [64, 9], replicated, may hold values from -3 to 3
- point_mix: bfloat16 [64, 64], replicated, may hold values from -1 to 1
- first_conv: bfloat16 [3, 3, 64, 64], replicated, may hold values from -0.375 to 0.375
- second_conv: bfloat16 [3, 3, 64, 64], replicated, may hold values from -0.375 to 0.375
- third_conv: bfloat16 [3, 3, 128, 64], replicated, may hold values from -0.375 to 0.375
- fourth_conv: bfloat16 [3, 3, 128, 128], replicated, may hold values from -0.25 to 0.25
- fifth_conv: bfloat16 [3, 3, 256, 128], replicated, may hold values from -0.25 to 0.25
- sixth_conv: bfloat16 [3, 3, 256, 256], replicated, may hold values from -0.1875 to 0.1875
- near_lift: bfloat16 [1, 1, 128, 64], replicated, may hold values from -1 to 1
- mid_lift: bfloat16 [2, 2, 128, 128], replicated, may hold values from -0.75 to 0.75
- far_lift: bfloat16 [4, 4, 128, 256], replicated, may hold values from -0.5 to 0.5
- biases: float32 [1408], replicated, may hold values from -1.5 to 1.5
Outputs:
- joined: bfloat16 [384, 256, 512], P(None, ('slab', 'row'), 'col'), parts along dimension 1
There are 2 independent parts, one for each index of `slab`. A program takes and returns all parts, laid end to end along the dimension named above; an argument that names none is the same for every part. Nothing has to cross between parts.
Inputs may be any that keep to these rules, and one draw needn't show every extreme that they name: `tile_count`: entry s * 16 + t counts the live slots that device s (row-major over row and col) holds for tile t (row-major over row and col); they are the first of that tile's group of 256 slots. In every draw some tile gets exactly 256 live slots from every device. `pillar_cell`: slot s holds cell r * 512 + c; every slot in a device's group for tile t lies in tile t, whose rows and columns are those of device t; a cell may appear in several slots, on one device or several. `point_count`: the valid points of a slot are its first ones.
All inputs are finite; a program needn't handle non-finite values.
Results may differ from a plain program's by a relative error of at most 0.0081.
Values may be sent and summed in bfloat16 or wider, within the bound.
A program may use at most 64 MiB of HBM per device.

v0:
```python
import functools

import jax
import jax.numpy as jnp
from jax import lax
from jax.experimental import pallas as pl
from jax.experimental.pallas import tpu as pltpu
from jax.sharding import PartitionSpec as P

ROWS_DEV = 16
COLS_DEV = 256
PACK = 4
HALF = 16
LANES = 4
SIDE = 16
TILE = 128


def prepare_kernel(embed_ref, mix_ref, bias_ref, w1_ref, w2_ref, b1_ref, b2_ref):
    mid, feat = embed_ref.shape
    chan = mix_ref.shape[0]
    wide = w1_ref.shape[2]
    lane = lax.broadcasted_iota(jnp.int32, (feat, wide), 1)
    spread = lane // HALF == lax.broadcasted_iota(jnp.int32, (feat, wide), 0)
    spread = jnp.where(spread, 1.0, 0.0).astype(jnp.bfloat16)
    full = jnp.dot(embed_ref[...], spread, preferred_element_type=jnp.float32)
    point = lax.broadcasted_iota(jnp.int32, (mid, wide), 1) % HALF
    for q in range(HALF // PACK):
        for p in range(PACK):
            part = jnp.where(point == q * PACK + p, full, 0.0)
            w1_ref[q, p * mid : (p + 1) * mid, :] = part.astype(jnp.bfloat16)
    w2_ref[...] = jnp.zeros_like(w2_ref)
    for p in range(PACK):
        w2_ref[p * chan : (p + 1) * chan, p * mid : (p + 1) * mid] = mix_ref[...]
    both = mid + chan
    column = jnp.broadcast_to(bias_ref[:, 0:both], (both, both)).T[:, 0:1]
    for p in range(PACK):
        b1_ref[p * mid : (p + 1) * mid, :] = column[0:mid]
    b2_ref[...] = column[mid:both]


def encode_kernel(
    x_ref, count_ref, cell_ref, w1_ref, w2_ref, b1_ref, b2_ref, out_ref, place_ref,
    send_ref, ssem, rsem, place_ssem, place_rsem
):
    feat, points, _ = x_ref.shape
    tiles, _, cap = count_ref.shape
    chan = b2_ref.shape[0]
    half = tiles // 2
    col_count = lax.axis_size("col")
    me = lax.axis_index("row") * col_count + lax.axis_index("col")

    def device_of(tile):
        return {"row": tile // col_count, "col": tile % col_count}

    def encode(tile, dest_ref):
        count = count_ref[tile]
        start = pl.multiple_of(tile * cap, cap)
        best = jnp.full((chan, cap), -jnp.inf, jnp.float32)
        for h in range(points // HALF):
            block = x_ref[:, h * HALF : (h + 1) * HALF, pl.ds(start, cap)]
            block = block.reshape(feat * HALF, cap)
            for q in range(HALF // PACK):
                hidden = jnp.dot(w1_ref[q], block, preferred_element_type=jnp.float32)
                hidden = jnp.maximum(hidden + b1_ref[...], 0.0).astype(jnp.bfloat16)
                second = jnp.dot(w2_ref[...], hidden, preferred_element_type=jnp.float32)
                for p in range(PACK):
                    j = h * HALF + q * PACK + p
                    part = second[p * chan : (p + 1) * chan]
                    best = jnp.maximum(best, jnp.where(count > j, part, -jnp.inf))
        vec = jnp.maximum(best + b2_ref[...], 0.0)
        dest_ref[tile] = vec.astype(jnp.bfloat16)

    def place_of(i, slot):
        tile = (me + i) % tiles
        return pltpu.make_async_remote_copy(
            src_ref=cell_ref.at[tile],
            dst_ref=place_ref.at[slot],
            send_sem=place_ssem.at[i],
            recv_sem=place_rsem.at[i],
            device_id=device_of(tile),
            device_id_type=pl.DeviceIdType.MESH,
        )

    def copy_of(i, slot):
        tile = (me + i) % tiles
        return pltpu.make_async_remote_copy(
            src_ref=send_ref.at[tile],
            dst_ref=out_ref.at[slot],
            send_sem=ssem.at[i],
            recv_sem=rsem.at[i],
            device_id=device_of(tile),
            device_id_type=pl.DeviceIdType.MESH,
        )

    barrier = pltpu.get_barrier_semaphore()

    def greet(i, carry):
        pl.semaphore_signal(
            barrier,
            inc=1,
            device_id=device_of((me + i) % tiles),
            device_id_type=pl.DeviceIdType.MESH,
        )
        return carry

    lax.fori_loop(1, tiles, greet, 0)
    pl.semaphore_wait(barrier, tiles - 1)

    def step(k, carry):
        i = half + (1 - 2 * (k % 2)) * ((k + 1) // 2)
        encode((me + i) % tiles, send_ref)
        copy_of(i, me).start()
        place_of(i, me).start()
        return carry

    lax.fori_loop(0, tiles - 1, step, 0, unroll=3)
    encode(me, out_ref)
    place_ref[me] = cell_ref[me]

    def finish(i, carry):
        copy_of(i, me).wait_send()
        place_of(i, me).wait_send()
        copy_of(i, (me - i + tiles) % tiles).wait_recv()
        place_of(i, (me - i + tiles) % tiles).wait_recv()
        return carry

    lax.fori_loop(1, tiles, finish, 0)


def encode_all(points, counts, cells, embed, mix, bias):
    feat = points.shape[0]
    tiles, _, cap = counts.shape
    mid, chan = embed.shape[0], mix.shape[0]
    vmem = pl.BlockSpec(memory_space=pltpu.VMEM)
    weights = pl.pallas_call(
        prepare_kernel,
        in_specs=[vmem] * 3,
        out_specs=[vmem] * 4,
        out_shape=[
            jax.ShapeDtypeStruct((HALF // PACK, PACK * mid, feat * HALF), jnp.bfloat16),
            jax.ShapeDtypeStruct((PACK * chan, PACK * mid), jnp.bfloat16),
            jax.ShapeDtypeStruct((PACK * mid, 1), jnp.float32),
            jax.ShapeDtypeStruct((chan, 1), jnp.float32),
        ],
        name="prepare",
    )(embed, mix, bias)
    return pl.pallas_call(
        encode_kernel,
        in_specs=[vmem] * 7,
        out_specs=[vmem, vmem],
        out_shape=[
            jax.ShapeDtypeStruct((tiles, chan, cap), jnp.bfloat16),
            jax.ShapeDtypeStruct((tiles, 1, cap), jnp.int32),
        ],
        scratch_shapes=[
            pltpu.VMEM((tiles, chan, cap), jnp.bfloat16),
            pltpu.SemaphoreType.DMA((tiles,)),
            pltpu.SemaphoreType.DMA((tiles,)),
            pltpu.SemaphoreType.DMA((tiles,)),
            pltpu.SemaphoreType.DMA((tiles,)),
        ],
        compiler_params=pltpu.CompilerParams(collective_id=7, has_side_effects=True),
        name="encode_send",
    )(points, counts, cells, *weights)


def scatter_kernel(cell_ref, vec_ref, out_ref, stage, *grids):
    tiles, _, cap = vec_ref.shape
    chan = out_ref.shape[1]
    for grid in grids:
        grid[...] = jnp.zeros_like(grid)

    def per_tile(t, carry):
        stage[...] = vec_ref[t, 0:chan, :].astype(jnp.float32).T
        unroll = 8

        def per_slot(s, inner):
            for k in range(unroll):
                cells = [cell_ref[t * cap + (s * unroll + k) * LANES + a] for a in range(LANES)]
                base = (s * unroll + k) * LANES
                olds = [grids[a][pl.ds(cells[a], 1), :] for a in range(LANES)]
                for a in range(LANES):
                    grids[a][pl.ds(cells[a], 1), :] = jnp.maximum(
                        olds[a], stage[pl.ds(base + a, 1), :]
                    )
            return inner

        return lax.fori_loop(0, cap // (LANES * unroll), per_slot, carry)

    lax.fori_loop(0, tiles, per_tile, 0)
    total = grids[0][...]
    for grid in grids[1:]:
        total = jnp.maximum(total, grid[...])
    out_ref[...] = total.astype(jnp.bfloat16)


def scatter_max(cells, vectors, chan):
    tiles, _, cap = vectors.shape
    area = ROWS_DEV * COLS_DEV
    return pl.pallas_call(
        scatter_kernel,
        in_specs=[
            pl.BlockSpec(memory_space=pltpu.SMEM),
            pl.BlockSpec(memory_space=pltpu.VMEM),
        ],
        out_specs=pl.BlockSpec(memory_space=pltpu.VMEM),
        out_shape=jax.ShapeDtypeStruct((area, chan), jnp.bfloat16),
        scratch_shapes=[pltpu.VMEM((cap, chan), jnp.float32)]
        + [pltpu.VMEM((area, chan), jnp.float32)] * LANES,
        name="scatter_max",
    )(cells, vectors)


def around(count_rows, count_cols):
    return [
        (dr, dc)
        for dr in (-1, 0, 1)
        for dc in (-1, 0, 1)
        if (dr, dc) != (0, 0) and (dr == 0 or count_rows > 1) and (dc == 0 or count_cols > 1)
    ]


def span_of(step, before, size, after):
    if step > 0:
        return slice(size - before, size), slice(0, before)
    if step < 0:
        return slice(0, after), slice(before + size, before + size + after)
    return slice(0, size), slice(before, before + size)


def halo_kernel(before, after, x_ref, ext_ref, send_sem, recv_sem, *packs):
    rows, cols, chan = x_ref.shape
    part = cols // 2
    packed = {}
    if packs:
        packed = {(1, 0): packs[0:2], (-1, 0): packs[2:4]}
        for (dr, dc), (source, _) in packed.items():
            row_from = span_of(dr, before, rows, after)[0]
            source[:, :, 0:chan] = x_ref[row_from, 0:part, :]
            source[:, :, chan : 2 * chan] = x_ref[row_from, part:cols, :]
    count_rows, count_cols = lax.axis_size("row"), lax.axis_size("col")
    my_row, my_col = lax.axis_index("row"), lax.axis_index("col")
    steps = around(count_rows, count_cols)

    def exists(dr, dc):
        row, col = my_row + dr, my_col + dc
        return (row >= 0) & (row < count_rows) & (col >= 0) & (col < count_cols)

    barrier = pltpu.get_barrier_semaphore()
    for dr, dc in steps:

        @pl.when(exists(dr, dc))
        def _():
            pl.semaphore_signal(
                barrier,
                inc=1,
                device_id={"row": my_row + dr, "col": my_col + dc},
                device_id_type=pl.DeviceIdType.MESH,
            )

    peers = sum(jnp.where(exists(dr, dc), 1, 0) for dr, dc in steps)
    pl.semaphore_wait(barrier, peers)

    def copy_of(place):
        dr, dc = steps[place]
        row_from, row_to = span_of(dr, before, rows, after)
        col_from, col_to = span_of(dc, SIDE, cols, SIDE)
        source, target = x_ref.at[row_from, col_from, :], ext_ref.at[row_to, col_to, :]
        if (dr, dc) in packed:
            source, target = packed[(dr, dc)]
        return pltpu.make_async_remote_copy(
            src_ref=source,
            dst_ref=target,
            send_sem=send_sem.at[place],
            recv_sem=recv_sem.at[place],
            device_id={"row": my_row + dr, "col": my_col + dc},
            device_id_type=pl.DeviceIdType.MESH,
        )

    for place, (dr, dc) in enumerate(steps):

        @pl.when(exists(dr, dc))
        def _():
            copy_of(place).start()

    ext_ref[before : before + rows, SIDE : SIDE + cols, :] = x_ref[...]
    for dr in (-1, 0, 1):
        for dc in (-1, 0, 1):
            if (dr, dc) == (0, 0):
                continue
            row_to = span_of(dr, before, rows, after)[1]
            col_to = span_of(dc, SIDE, cols, SIDE)[1]
            shape = (row_to.stop - row_to.start, col_to.stop - col_to.start, chan)

            @pl.when(jnp.logical_not(exists(-dr, -dc)))
            def _():
                ext_ref[row_to, col_to, :] = jnp.zeros(shape, ext_ref.dtype)

    for place, (dr, dc) in enumerate(steps):

        @pl.when(exists(dr, dc))
        def _():
            copy_of(place).wait_send()

        @pl.when(exists(-dr, -dc))
        def _():
            copy_of(place).wait_recv()
            if (dr, dc) in packed:
                target = packed[(dr, dc)][1]
                row_to = span_of(dr, before, rows, after)[1]
                ext_ref[row_to, SIDE : SIDE + part, :] = target[:, :, 0:chan]
                ext_ref[row_to, SIDE + part : SIDE + cols, :] = target[:, :, chan : 2 * chan]


def with_halo(block, before, after, call_id):
    rows, cols, chan = block.shape
    count = len(around(lax.axis_size("row"), lax.axis_size("col")))
    packs = []
    if 2 * chan == TILE and lax.axis_size("row") > 1:
        for depth in (before, before, after, after):
            packs.append(pltpu.VMEM((depth, cols // 2, TILE), block.dtype))
    return pl.pallas_call(
        functools.partial(halo_kernel, before, after),
        in_specs=[pl.BlockSpec(memory_space=pltpu.VMEM)],
        out_specs=pl.BlockSpec(memory_space=pltpu.VMEM),
        out_shape=jax.ShapeDtypeStruct(
            (rows + before + after, cols + 2 * SIDE, chan), block.dtype
        ),
        scratch_shapes=[
            pltpu.SemaphoreType.DMA((count,)),
            pltpu.SemaphoreType.DMA((count,)),
        ]
        + packs,
        compiler_params=pltpu.CompilerParams(collective_id=call_id, has_side_effects=True),
        name=f"halo_{call_id}",
    )(block)


def level_kernel(
    stride, factor, bias_at, ext_ref, wa_ref, wb_ref, bias_ref, out_ref, wide_ref,
    ta, tb, stage_a, cat_a, stage_b, cat_b, wide
):
    ext_rows, ext_cols, chan_in = ext_ref.shape
    rows, cols, chan = out_ref.shape
    mid_rows, mid_cols, _ = cat_b.shape
    edge = SIDE // stride
    for w_ref, t_ref in ((wa_ref, ta), (wb_ref, tb)):
        deep = w_ref.shape[3]
        for u in range(3):
            for v in range(3):
                flip = w_ref[u, v].astype(jnp.float32).T
                t_ref[u, v * deep : (v + 1) * deep, :] = flip.astype(jnp.bfloat16)
    for stage in (stage_a, stage_b):
        stage[0:8, :] = jnp.zeros((8, stage.shape[1]), jnp.float32)
        stage[stage.shape[0] - 8 :, :] = jnp.zeros((8, stage.shape[1]), jnp.float32)

    wide[...] = jnp.zeros_like(wide)

    def gather(stage, values, count, step):
        stage[8 : 8 + values.shape[0], :] = values
        if step == 1:
            parts = [stage[7 + v : 7 + v + count, :] for v in range(3)]
        else:
            parts = [stage[pl.ds(7 + v, count, stride=step), :] for v in range(3)]
        return jnp.concatenate(parts, axis=1).astype(jnp.bfloat16)

    def first(r, carry):
        cat_a[r] = gather(stage_a, ext_ref[r].astype(jnp.float32), mid_cols, stride)
        return carry

    lax.fori_loop(0, ext_rows, first, 0, unroll=4)

    col = lax.broadcasted_iota(jnp.int32, (mid_cols, chan), 0) - edge
    col = col + lax.axis_index("col") * cols
    col_good = (col >= 0) & (col < cols * lax.axis_size("col"))
    row_base = lax.axis_index("row") * rows
    row_limit = rows * lax.axis_size("row")

    def second(i, carry):
        total = jnp.broadcast_to(bias_ref[:, bias_at : bias_at + chan], (mid_cols, chan))
        for u in range(3):
            total = total + jnp.dot(
                cat_a[stride * i + u], ta[u], preferred_element_type=jnp.float32
            )
        total = jnp.maximum(total, 0.0).astype(jnp.bfloat16).astype(jnp.float32)
        row = row_base + i - 1
        total = jnp.where(col_good & (row >= 0) & (row < row_limit), total, 0.0)
        cat_b[i] = gather(stage_b, total, mid_cols, 1)
        return carry

    lax.fori_loop(0, mid_rows, second, 0, unroll=4)

    def third(i, carry):
        total = jnp.broadcast_to(
            bias_ref[:, bias_at + chan : bias_at + 2 * chan], (mid_cols, chan)
        )
        for u in range(3):
            total = total + jnp.dot(cat_b[i + u], tb[u], preferred_element_type=jnp.float32)
        total = jnp.maximum(total, 0.0)
        total = total[edge : edge + cols]
        out_ref[i] = total.astype(jnp.bfloat16)
        if factor > 1:
            parts = chan // TILE
            for b in range(factor):
                for k in range(parts):
                    piece = total[:, k * TILE : (k + 1) * TILE]
                    wide[b * parts + k, pl.ds(b, cols, stride=factor), :] = piece
            for k in range(factor * parts):
                wide_ref[i, :, k * TILE : (k + 1) * TILE] = wide[k].astype(jnp.bfloat16)
        return carry

    lax.fori_loop(0, rows, third, 0, unroll=4)


def level(block, kernel_a, kernel_b, bias, bias_at, stride, factor, call_id):
    rows, cols, chan_in = block.shape
    before, after = (2, 2) if stride == 1 else (3, 2)
    ext = with_halo(block, before, after, call_id)
    chan = kernel_a.shape[2]
    rows_out, cols_out = rows // stride, cols // stride
    mid_rows, mid_cols = rows_out + 2, ext.shape[1] // stride
    vmem = pl.BlockSpec(memory_space=pltpu.VMEM)
    wide_shape = (rows_out, cols_out * factor, chan * factor) if factor > 1 else (1, 16, 128)
    return pl.pallas_call(
        functools.partial(level_kernel, stride, factor, bias_at),
        in_specs=[vmem] * 4,
        out_specs=[vmem, vmem],
        out_shape=[
            jax.ShapeDtypeStruct((rows_out, cols_out, chan), jnp.bfloat16),
            jax.ShapeDtypeStruct(wide_shape, jnp.bfloat16),
        ],
        scratch_shapes=[
            pltpu.VMEM((3, 3 * chan_in, chan), jnp.bfloat16),
            pltpu.VMEM((3, 3 * chan, chan), jnp.bfloat16),
            pltpu.VMEM((ext.shape[1] + 16, chan_in), jnp.float32),
            pltpu.VMEM((ext.shape[0], mid_cols, 3 * chan_in), jnp.bfloat16),
            pltpu.VMEM((mid_cols + 16, chan), jnp.float32),
            pltpu.VMEM((mid_rows, mid_cols, 3 * chan), jnp.bfloat16),
            pltpu.VMEM((factor * chan // TILE, cols_out * factor, TILE) if factor > 1 else (1, 8, TILE), jnp.float32),
        ],
        name=f"level_{call_id}",
    )(ext, kernel_a, kernel_b, bias)


def lift_layer(wide, kernel, bias_vec):
    factor = kernel.shape[0]
    rows, cols, depth = wide.shape
    weight = jnp.transpose(kernel, (2, 0, 1, 3)).reshape(kernel.shape[2], factor, depth)
    product = jnp.einsum("oak,ijk->oiaj", weight, wide, preferred_element_type=jnp.float32)
    product = product.reshape(kernel.shape[2], rows * factor, cols)
    return jax.nn.relu(product + bias_vec[:, None, None]).astype(jnp.bfloat16)


def on_device(
    points,
    pillar_cell,
    point_count,
    tile_count,
    point_embed,
    point_mix,
    first_conv,
    second_conv,
    third_conv,
    fourth_conv,
    fifth_conv,
    sixth_conv,
    near_lift,
    mid_lift,
    far_lift,
    biases,
):
    extents = [
        point_embed.shape[0],
        point_mix.shape[0],
        first_conv.shape[2],
        second_conv.shape[2],
        third_conv.shape[2],
        fourth_conv.shape[2],
        fifth_conv.shape[2],
        sixth_conv.shape[2],
        near_lift.shape[2],
        mid_lift.shape[2],
        far_lift.shape[2],
    ]
    pieces = []
    offset = 0
    for extent in extents:
        pieces.append(biases[offset : offset + extent])
        offset += extent
    tile_num = tile_count.shape[0]
    capacity = points.shape[2] // tile_num
    ncols_all = COLS_DEV * lax.axis_size("col")
    live_slot = lax.broadcasted_iota(jnp.int32, (tile_num, capacity), 1) < tile_count[:, None]
    live_points = jnp.where(live_slot, point_count.reshape(tile_num, capacity), 0)
    row_local = pillar_cell // ncols_all % ROWS_DEV
    local_cell = row_local * COLS_DEV + pillar_cell % COLS_DEV
    lead = biases.reshape(1, -1)
    vectors, places = encode_all(
        points,
        live_points.reshape(tile_num, 1, capacity),
        local_cell.reshape(tile_num, 1, capacity),
        point_embed,
        point_mix,
        lead,
    )
    chan = point_mix.shape[0]
    cells = places.reshape(-1)
    bev = scatter_max(cells, vectors, chan).reshape(ROWS_DEV, COLS_DEV, chan)
    level_one, _ = level(bev, first_conv, second_conv, lead, sum(extents[:2]), 1, 1, 0)
    level_two, wide_two = level(
        level_one, third_conv, fourth_conv, lead, sum(extents[:4]), 2, mid_lift.shape[0], 1
    )
    _, wide_three = level(
        level_two, fifth_conv, sixth_conv, lead, sum(extents[:6]), 2, far_lift.shape[0], 2
    )
    near = lift_layer(level_one, near_lift, pieces[8])
    middle = lift_layer(wide_two, mid_lift, pieces[9])
    distant = lift_layer(wide_three, far_lift, pieces[10])
    return jnp.concatenate([near, middle, distant], axis=0)


def solution(mesh):
    return jax.shard_map(
        on_device,
        mesh=mesh,
        in_specs=(
            P(None, None, ("slab", "row", "col")),
            P(("slab", "row", "col")),
            P(("slab", "row", "col")),
            P(("slab", "row", "col")),
            P(),
            P(),
            P(),
            P(),
            P(),
            P(),
            P(),
            P(),
            P(),
            P(),
            P(),
            P(),
        ),
        out_specs=P(None, ("slab", "row"), "col"),
        check_vma=False,
    )
```

profile of v0, /device:TPU:9, one launch (start us, length us, event | category | flops | bytes accessed | tf_op | source)
XLA Modules:
  0.0 104.2 jit_solution(10138271757387293861)
XLA Ops:
  0.0 0.0 copy-start
  0.0 1.3 %reshape.76.bias_ref = f32[1,1408]{1,0:T(1,128)} reshape(f32[1408]{0:T(1024)} %param.31) | data formatting | bytes 11264 | tf_op jit(solution)/shard_map/reshape | solution.py:498
  1.3 1.4 %copy.21.embed_ref = bf16[64,9]{1,0:T(8,128)(2,1)} copy(bf16[64,9]{0,1:T(8,128)(2,1)} %param.20) | data formatting | bytes 2304 | tf_op args[4]
  2.7 1.8 %prepare.1 = (bf16[4,256,144]{2,1,0:T(8,128)(2,1)}, bf16[256,256]{1,0:T(8,128)(2,1)}, f32[256,1]{1,0:T(8,128)}, f32[64,1]{1,0:T(8,128)}) custom-call(bf16[64,9]{1,0:T(8,128)(2,1)} %copy.21.embed_ref, bf16[64,64]{1,0:T(8,128)(2,1)} %mix_ref.1, f32[1,1408]{1,0:T(1,128)} %reshape.76.bias_ref), custom_call_target="tpu_custom_call" | custom-call | tf_op jit(solution)/shard_map/prepare/pallas_call | solution.py:136
  4.4 1.3 %fusion.13 = s32[4096]{0:T(1024)} fusion(s32[4096]{0:T(1024)} %param.17), kind=kLoop, calls=%fused_computation.27 | loop fusion | flops 147456 | bytes 32768 | tf_op jit(solution)/shard_map/add | solution.py:497
  5.8 1.4 %compare_select_fusion.count_ref = s32[16,1,256]{2,1,0:T(1,128)} fusion(s32[16,1,256]{2,1,0:T(1,128)} %bitcast.63, s32[16]{0:T(128)} %param.19), kind=kLoop, calls=%fused_computation.14 | loop fusion | flops 8192 | bytes 32832 | tf_op jit(solution)/shard_map/jit(_where)/select_n | solution.py:495
  7.2 22.6 %encode_send.1 = (bf16[16,64,256]{2,1,0:T(8,128)(2,1)}, s32[16,1,256]{2,1,0:T(1,128)}) custom-call(bf16[9,32,4096]{2,1,0:T(8,128)(2,1)} %x_ref.1, s32[16,1,256]{2,1,0:T(1,128)} %compare_select_fusion.count_ref, s32[16,1,256]{2,1,0:T(1,128)} %bitcast.61, bf16[4,256,144]{2,1,0:T(8,128)(2,1)} %get-tuple-element.15.w1_ref, ...), custom_call_target="tpu_custom_call" | custom-call | tf_op jit(solution)/shard_map/encode_send/pallas_call | solution.py:148
  29.8 10.0 %scatter_max.1 = bf16[4096,64]{1,0:T(8,128)(2,1)} custom-call(s32[4096]{0:T(1024)} %bitcast.62, bf16[16,64,256]{2,1,0:T(8,128)(2,1)} %get-tuple-element.20.vec_ref), custom_call_target="tpu_custom_call" | custom-call | tf_op jit(solution)/shard_map/scatter_max/pallas_call | solution.py:201
  39.7 8.7 %halo_0.1.ext_ref = bf16[20,288,64]{2,1,0:T(8,128)(2,1)} custom-call(bf16[16,256,64]{2,1,0:T(8,128)(2,1)} %bitcast.58), custom_call_target="tpu_custom_call" | custom-call | tf_op jit(solution)/shard_map/halo_0/pallas_call | solution.py:323
  48.5 0.0 copy-start.4
  48.5 10.9 %level_0.1 = (bf16[16,256,64]{2,1,0:T(8,128)(2,1)}, bf16[1,16,128]{2,1,0:T(8,128)(2,1)}) custom-call(bf16[20,288,64]{2,1,0:T(8,128)(2,1)} %halo_0.1.ext_ref, bf16[3,3,64,64]{3,2,1,0:T(8,128)(2,1)} %wa_ref.3, bf16[3,3,64,64]{3,2,1,0:T(8,128)(2,1)} %wb_ref.3, f32[1,1408]{1,0:T(1,128)} %reshape.76.bias_ref), custom_call_target="tpu_custom_call" | custom-call | tf_op jit(solution)/shard_map/level_0/pallas_call | solution.py:425
  59.4 10.2 %halo_1.1.ext_ref = bf16[21,288,64]{2,1,0:T(8,128)(2,1)} custom-call(bf16[16,256,64]{2,1,0:T(8,128)(2,1)} %get-tuple-element.21.x_ref), custom_call_target="tpu_custom_call" | custom-call | tf_op jit(solution)/shard_map/halo_1/pallas_call | solution.py:323
  69.7 0.0 copy-done.4
  69.7 0.9 copy.23.wa_ref
  70.6 0.0 copy-start.3
  70.6 6.5 %level_1.1 = (bf16[8,128,128]{2,1,0:T(8,128)(2,1)}, bf16[8,256,256]{2,1,0:T(8,128)(2,1)}) custom-call(bf16[21,288,64]{2,1,0:T(8,128)(2,1)} %halo_1.1.ext_ref, bf16[3,3,128,64]{3,2,1,0:T(8,128)(2,1)} %copy.23.wa_ref, bf16[3,3,128,128]{3,2,1,0:T(8,128)(2,1)} %wb_ref.4, f32[1,1408]{1,0:T(1,128)} %reshape.76.bias_ref), custom_call_target="tpu_custom_call" | custom-call | tf_op jit(solution)/shard_map/level_1/pallas_call | solution.py:425
  77.0 9.4 %halo_2.1.ext_ref = bf16[13,160,128]{2,1,0:T(8,128)(2,1)} custom-call(bf16[8,128,128]{2,1,0:T(8,128)(2,1)} %get-tuple-element.23.x_ref), custom_call_target="tpu_custom_call" | custom-call | tf_op jit(solution)/shard_map/halo_2/pallas_call | solution.py:323
  86.5 6.3 %level_2.1 = (bf16[4,64,256]{2,1,0:T(8,128)(2,1)}, bf16[4,256,1024]{2,1,0:T(8,128)(2,1)}) custom-call(bf16[13,160,128]{2,1,0:T(8,128)(2,1)} %halo_2.1.ext_ref, bf16[3,3,256,128]{3,2,1,0:T(8,128)(2,1)} %wa_ref.4, bf16[3,3,256,256]{3,2,1,0:T(8,128)(2,1)} %wb_ref.5, f32[1,1408]{1,0:T(1,128)} %reshape.76.bias_ref), custom_call_target="tpu_custom_call" | custom-call | tf_op jit(solution)/shard_map/level_2/pallas_call | solution.py:425
  92.8 0.0 copy-done.3
  92.8 1.3 %copy.26 = bf16[4,4,128,256]{2,3,1,0:T(8,128)(2,1)} copy(bf16[4,4,128,256]{3,2,1,0:T(8,128)(2,1)S(1)} %copy-done.3) | data formatting | bytes 2097152 | tf_op args[14]
  94.1 0.0 copy-start.5
  94.1 0.0 copy-start.2
  94.1 3.2 %fusion.2 = f32[4,256,128,4]{1,2,3,0:T(8,128)S(1)} fusion(bf16[128,4,1024,1]{0,2,1,3:T(8,128)(2,1)} %bitcast.59, bf16[4,256,1024]{2,1,0:T(8,128)(2,1)} %get-tuple-element.24), kind=kOutput, calls=%fused_computation.4 | convolution fusion | flops 1073741824 | bytes 5242880 | tf_op jit(solution)/shard_map/oak,ijk->oiaj/dot_general | solution.py:450
  97.4 0.0 copy-done.5
  97.4 0.1 copy.24
  97.5 0.0 copy-done.2
  97.5 0.5 fusion.8
  98.0 0.8 fusion.16
  98.8 0.0 copy-start.1
  98.8 0.6 fusion.1
  99.5 0.0 copy-done
  99.5 0.6 copy-done.1
  100.0 0.5 fusion.7
  100.5 0.3 pad_maximum_fusion
  100.8 3.4 %copy.28 = bf16[384,16,256]{2,1,0:T(8,128)(2,1)} copy(bf16[384,16,256]{2,0,1:T(8,128)(2,1)S(1)} %pad_maximum_fusion) | data formatting | bytes 6291456 | tf_op jit(solution)/shard_map/concatenate | solution.py:520
Async XLA Ops:
  0.0 99.5 %copy-start = (bf16[1,1,128,64]{2,3,1,0:T(8,128)(2,1)S(1)}, bf16[1,1,128,64]{2,3,1,0:T(8,128)(2,1)}, u32[]{:S(2)}) copy-start(bf16[1,1,128,64]{2,3,1,0:T(8,128)(2,1)} %param.28) | copy-start | bytes 49156
  48.5 21.2 %copy-start.4 = (bf16[3,3,128,64]{2,3,1,0:T(8,128)(2,1)S(1)}, bf16[3,3,128,64]{2,3,1,0:T(8,128)(2,1)}, u32[]{:S(2)}) copy-start(bf16[3,3,128,64]{2,3,1,0:T(8,128)(2,1)} %param.24) | copy-start | bytes 442372
  70.6 22.2 %copy-start.3 = (bf16[4,4,128,256]{3,2,1,0:T(8,128)(2,1)S(1)}, bf16[4,4,128,256]{3,2,1,0:T(8,128)(2,1)}, u32[]{:S(2)}) copy-start(bf16[4,4,128,256]{3,2,1,0:T(8,128)(2,1)} %param.30) | copy-start | bytes 3145732
  94.1 3.3 %copy-start.5 = (bf16[2,2,128,128]{3,2,1,0:T(8,128)(2,1)S(1)}, bf16[2,2,128,128]{3,2,1,0:T(8,128)(2,1)}, u32[]{:S(2)}) copy-start(bf16[2,2,128,128]{3,2,1,0:T(8,128)(2,1)} %param.29) | copy-start | bytes 393220
  94.1 3.4 %copy-start.2 = (bf16[8,256,256]{2,1,0:T(8,128)(2,1)S(1)}, bf16[8,256,256]{2,1,0:T(8,128)(2,1)}, u32[]{:S(2)}) copy-start(bf16[8,256,256]{2,1,0:T(8,128)(2,1)} %get-tuple-element.22) | copy-start | bytes 3145732
  98.8 1.2 %copy-start.1 = (bf16[16,256,64]{2,1,0:T(8,128)(2,1)S(1)}, bf16[16,256,64]{2,1,0:T(8,128)(2,1)}, u32[]{:S(2)}) copy-start(bf16[16,256,64]{2,1,0:T(8,128)(2,1)} %get-tuple-element.21.x_ref) | copy-start | bytes 1572868
where the time goes:
time: 105 us; the launch traced here: 104 us
  Pallas kernels  86.4 us (82%)
  local copies, waits for them, and re-layouts  9.85 us (9%)
  matrix products  4.21 us (4%)
  other arithmetic  3.63 us (3%)
    pallas_call x3, Pallas kernels, with_halo(): pl.pallas_call(functools.partial(halo_kernel, before, after), in_specs=[p...  28.4 us
    pallas_call x3, Pallas kernels, level(): pl.pallas_call(functools.partial(level_kernel, stride, factor, bias_at),...  23.7 us
    pallas_call x1, Pallas kernels, encode_all(): pl.pallas_call(encode_kernel, in_specs=[vmem] * 7, out_specs=[vmem, vmem]...  22.6 us
    pallas_call x1, Pallas kernels, scatter_max(): pl.pallas_call(scatter_kernel, in_specs=[pl.BlockSpec(memory_space=pltpu....  10 us
    unnamed x16, local copies, waits for them, and re-layouts  4.31 us
    dot_general x3, matrix products, lift_layer(): jnp.einsum('oak,ijk->oiaj', weight, wide, preferred_element_type=jnp.floa...  4.21 us
    concatenate x1, local copies, waits for them, and re-layouts, on_device(): return jnp.concatenate([near, middle, distant], axis=0)  3.44 us

commit v1 on v0

v1 whole, which is shorter than its diff:
```python
import jax
import jax.numpy as jnp
from jax import lax
from jax.experimental import pallas as pl
from jax.experimental.pallas import tpu as pltpu
from jax.sharding import PartitionSpec as P

ROWS_DEV = 16
COLS_DEV = 256
PACK = 4
HALF = 16
LANES = 4
SIDE = 16
TILE = 128


def encode_kernel(
    x_ref, count_ref, cell_ref, embed_ref, mix_ref, bias_ref, live_ref, out_ref, place_ref,
    send_ref, place_send, w1_ref, w2_ref, b1_ref, b2_ref, ssem, rsem, place_ssem, place_rsem
):
    feat, points, _ = x_ref.shape
    tiles, _, cap = count_ref.shape
    chan, mid = mix_ref.shape
    half = tiles // 2
    col_count = lax.axis_size("col")
    me = lax.axis_index("row") * col_count + lax.axis_index("col")

    def device_of(tile):
        return {"row": tile // col_count, "col": tile % col_count}

    barrier = pltpu.get_barrier_semaphore()

    def greet(i, carry):
        pl.semaphore_signal(
            barrier,
            inc=1,
            device_id=device_of((me + i) % tiles),
            device_id_type=pl.DeviceIdType.MESH,
        )
        return carry

    lax.fori_loop(1, tiles, greet, 0)

    wide = feat * HALF
    lane = lax.broadcasted_iota(jnp.int32, (feat, wide), 1)
    spread = lane // HALF == lax.broadcasted_iota(jnp.int32, (feat, wide), 0)
    spread = jnp.where(spread, 1.0, 0.0).astype(jnp.bfloat16)
    full = lax.dot_general(
        embed_ref[...], spread, (((0,), (0,)), ((), ())), preferred_element_type=jnp.float32
    )
    point = lax.broadcasted_iota(jnp.int32, (mid, wide), 1) % HALF
    for q in range(HALF // PACK):
        for p in range(PACK):
            part = jnp.where(point == q * PACK + p, full, 0.0)
            w1_ref[q, p * mid : (p + 1) * mid, :] = part.astype(jnp.bfloat16)
    w2_ref[...] = jnp.zeros_like(w2_ref)
    for p in range(PACK):
        w2_ref[p * chan : (p + 1) * chan, p * mid : (p + 1) * mid] = mix_ref[...]
    both = mid + chan
    column = jnp.broadcast_to(bias_ref[0:1, :], (both, both)).T[:, 0:1]
    for p in range(PACK):
        b1_ref[p * mid : (p + 1) * mid, :] = column[0:mid]
    b2_ref[...] = column[mid:both]
    cell = cell_ref[...]
    row = cell // (COLS_DEV * col_count) % ROWS_DEV
    place_send[...] = row * COLS_DEV + cell % COLS_DEV

    def encode(tile, dest_ref):
        slot = lax.broadcasted_iota(jnp.int32, (1, cap), 1)
        count = jnp.where(slot < live_ref[tile], count_ref[tile], 0)
        start = pl.multiple_of(tile * cap, cap)
        best = jnp.full((chan, cap), -jnp.inf, jnp.float32)
        for h in range(points // HALF):
            block = x_ref[:, h * HALF : (h + 1) * HALF, pl.ds(start, cap)]
            block = block.reshape(feat * HALF, cap)
            for q in range(HALF // PACK):
                hidden = jnp.dot(w1_ref[q], block, preferred_element_type=jnp.float32)
                hidden = jnp.maximum(hidden + b1_ref[...], 0.0).astype(jnp.bfloat16)
                second = jnp.dot(w2_ref[...], hidden, preferred_element_type=jnp.float32)
                for p in range(PACK):
                    j = h * HALF + q * PACK + p
                    part = second[p * chan : (p + 1) * chan]
                    best = jnp.maximum(best, jnp.where(count > j, part, -jnp.inf))
        vec = jnp.maximum(best + b2_ref[...], 0.0)
        dest_ref[tile] = vec.astype(jnp.bfloat16)

    def place_of(i, slot):
        tile = (me + i) % tiles
        return pltpu.make_async_remote_copy(
            src_ref=place_send.at[tile],
            dst_ref=place_ref.at[slot],
            send_sem=place_ssem.at[i],
            recv_sem=place_rsem.at[i],
            device_id=device_of(tile),
            device_id_type=pl.DeviceIdType.MESH,
        )

    def copy_of(i, slot):
        tile = (me + i) % tiles
        return pltpu.make_async_remote_copy(
            src_ref=send_ref.at[tile],
            dst_ref=out_ref.at[slot],
            send_sem=ssem.at[i],
            recv_sem=rsem.at[i],
            device_id=device_of(tile),
            device_id_type=pl.DeviceIdType.MESH,
        )

    pl.semaphore_wait(barrier, tiles - 1)

    def step(k, carry):
        i = half + (1 - 2 * (k % 2)) * ((k + 1) // 2)
        encode((me + i) % tiles, send_ref)
        copy_of(i, me).start()
        place_of(i, me).start()
        return carry

    lax.fori_loop(0, tiles - 1, step, 0, unroll=3)
    encode(me, out_ref)
    place_ref[me] = place_send[me]

    def finish(i, carry):
        copy_of(i, me).wait_send()
        place_of(i, me).wait_send()
        copy_of(i, (me - i + tiles) % tiles).wait_recv()
        place_of(i, (me - i + tiles) % tiles).wait_recv()
        return carry

    lax.fori_loop(1, tiles, finish, 0)


def encode_all(points, counts, cells, live, embed, mix, bias):
    feat = points.shape[0]
    tiles, _, cap = counts.shape
    chan, mid = mix.shape
    vmem = pl.BlockSpec(memory_space=pltpu.VMEM)
    return pl.pallas_call(
        encode_kernel,
        in_specs=[vmem] * 6 + [pl.BlockSpec(memory_space=pltpu.SMEM)],
        out_specs=[vmem, vmem],
        out_shape=[
            jax.ShapeDtypeStruct((tiles, chan, cap), jnp.bfloat16),
            jax.ShapeDtypeStruct((tiles, 1, cap), jnp.int32),
        ],
        scratch_shapes=[
            pltpu.VMEM((tiles, chan, cap), jnp.bfloat16),
            pltpu.VMEM((tiles, 1, cap), jnp.int32),
            pltpu.VMEM((HALF // PACK, PACK * mid, feat * HALF), jnp.bfloat16),
            pltpu.VMEM((PACK * chan, PACK * mid), jnp.bfloat16),
            pltpu.VMEM((PACK * mid, 1), jnp.float32),
            pltpu.VMEM((chan, 1), jnp.float32),
            pltpu.SemaphoreType.DMA((tiles,)),
            pltpu.SemaphoreType.DMA((tiles,)),
            pltpu.SemaphoreType.DMA((tiles,)),
            pltpu.SemaphoreType.DMA((tiles,)),
        ],
        compiler_params=pltpu.CompilerParams(collective_id=7, has_side_effects=True),
        name="encode_send",
    )(points, counts, cells, embed, mix, bias, live)


def scatter_kernel(cell_ref, vec_ref, out_ref, stage, *grids):
    tiles, chan, cap = vec_ref.shape
    area = out_ref.shape[0]
    for grid in grids:
        grid[...] = jnp.zeros_like(grid)
    lanes = len(grids)
    first_half = lax.broadcasted_iota(jnp.int32, (cap, 2 * chan), 1) < chan

    def per_tile(t, carry):
        twice = vec_ref[t].astype(jnp.float32)
        twice = jnp.concatenate([twice, twice], axis=0).T
        stage[0:cap, :] = jnp.where(first_half, twice, 0.0)
        stage[cap : 2 * cap, :] = jnp.where(first_half, 0.0, twice)
        unroll = 32 // lanes

        def per_slot(s, inner):
            for k in range(unroll):
                base = (s * unroll + k) * lanes
                cells = [cell_ref[t * cap + base + a] for a in range(lanes)]
                pairs = [lax.shift_right_logical(cell, 1) for cell in cells]
                rows = [base + a + (cells[a] & 1) * cap for a in range(lanes)]
                olds = [grids[a][pl.ds(pairs[a], 1), :] for a in range(lanes)]
                for a in range(lanes):
                    grids[a][pl.ds(pairs[a], 1), :] = jnp.maximum(
                        olds[a], stage[pl.ds(rows[a], 1), :]
                    )
            return inner

        return lax.fori_loop(0, cap // (lanes * unroll), per_slot, carry)

    lax.fori_loop(0, tiles, per_tile, 0)
    total = grids[0][...]
    for grid in grids[1:]:
        total = jnp.maximum(total, grid[...])
    out_ref[...] = total.astype(jnp.bfloat16)


def scatter_max(cells, vectors):
    tiles, chan, cap = vectors.shape
    area = ROWS_DEV * COLS_DEV // 2
    return pl.pallas_call(
        scatter_kernel,
        in_specs=[
            pl.BlockSpec(memory_space=pltpu.SMEM),
            pl.BlockSpec(memory_space=pltpu.VMEM),
        ],
        out_specs=pl.BlockSpec(memory_space=pltpu.VMEM),
        out_shape=jax.ShapeDtypeStruct((area, 2 * chan), jnp.bfloat16),
        scratch_shapes=[pltpu.VMEM((2 * cap, 2 * chan), jnp.float32)]
        + [pltpu.VMEM((area, 2 * chan), jnp.float32)] * LANES,
        name="scatter_max",
    )(cells, vectors)


STEPS = [(dr, dc) for dr in (1, -1) for dc in (0, 1, -1)] + [(0, 1), (0, -1)]


class Halo:
    def __init__(self, stage, own, top, bottom, left, right, send_sem, recv_sem):
        self.stage, self.own = stage, own
        self.top, self.bottom, self.left, self.right = top, bottom, left, right
        self.send_sem, self.recv_sem = send_sem, recv_sem
        self.rows, self.width, _ = own.shape
        self.before, self.after = top.shape[0], bottom.shape[0]
        self.count_rows, self.count_cols = lax.axis_size("row"), lax.axis_size("col")
        self.my_row, self.my_col = lax.axis_index("row"), lax.axis_index("col")
        self.steps = [
            (dr, dc)
            for dr, dc in STEPS
            if (dr == 0 or self.count_rows > 1) and (dc == 0 or self.count_cols > 1)
        ]

    def exists(self, dr, dc):
        row, col = self.my_row + dr, self.my_col + dc
        return (row >= 0) & (row < self.count_rows) & (col >= 0) & (col < self.count_cols)

    def peer(self, dr, dc):
        return {"row": self.my_row + dr, "col": self.my_col + dc}

    def clear(self):
        for ref in (self.top, self.bottom, self.left, self.right):
            ref[...] = jnp.zeros_like(ref)

    def copy_of(self, place):
        dr, dc = self.steps[place]
        before, rows, after = self.before, self.rows, self.after
        row_from = {1: slice(rows - before, rows), 0: slice(0, rows), -1: slice(0, after)}[dr]
        col_from = {1: slice(self.width - SIDE, self.width), 0: slice(0, self.width), -1: slice(0, SIDE)}[dc]
        row_to = {
            1: slice(0, before),
            0: slice(before, before + rows),
            -1: slice(before + rows, before + rows + after),
        }[dr]
        if dc == 0:
            target = self.top if dr == 1 else self.bottom
        else:
            target = (self.left if dc == 1 else self.right).at[row_to]
        return pltpu.make_async_remote_copy(
            src_ref=self.own.at[row_from, col_from, :],
            dst_ref=target,
            send_sem=self.send_sem.at[self.stage, place],
            recv_sem=self.recv_sem.at[self.stage, place],
            device_id=self.peer(dr, dc),
            device_id_type=pl.DeviceIdType.MESH,
        )

    def each(self, keep, sign, action):
        for place, (dr, dc) in enumerate(self.steps):
            if keep(dr, dc):

                @pl.when(self.exists(sign * dr, sign * dc))
                def _():
                    action(self.copy_of(place))

    def start(self, keep):
        self.each(keep, 1, lambda copy: copy.start())

    def wait_send(self):
        self.each(lambda dr, dc: True, 1, lambda copy: copy.wait_send())

    def wait_recv(self, keep):
        self.each(keep, -1, lambda copy: copy.wait_recv())


def across(dr, dc):
    return dr != 0


def beside(dr, dc):
    return dr == 0


def levels_kernel(
    bev_ref, w1a_ref, w1b_ref, w2a_ref, w2b_ref, w3a_ref, w3b_ref, bias_ref,
    one_ref, two_ref, three_ref,
    top0, bottom0, left0, right0, top1, bottom1, left1, right1, top2, bottom2, left2, right2,
    send_sem, recv_sem,
    t1a, t1b, t2a, t2b, t3a, t3b, cat1a, cat1b, cat2e, cat2o, cat2b, cat3e, cat3o, cat3b,
    stage, stage3, stage4,
):
    rows1, pairs, _ = bev_ref.shape
    rows2, cols2, chan2 = two_ref.shape
    rows3, cols3, chan3 = three_ref.shape
    chan1 = w1a_ref.shape[2]
    mid1 = pairs + 16
    mid3 = cols3 + 16
    zero = Halo(0, bev_ref, top0, bottom0, left0, right0, send_sem, recv_sem)
    one = Halo(1, one_ref, top1, bottom1, left1, right1, send_sem, recv_sem)
    two = Halo(2, two_ref, top2, bottom2, left2, right2, send_sem, recv_sem)
    for halo in (zero, one, two):
        halo.clear()
    barrier = pltpu.get_barrier_semaphore()
    for dr, dc in zero.steps:

        @pl.when(zero.exists(dr, dc))
        def _():
            pl.semaphore_signal(
                barrier, inc=1, device_id=zero.peer(dr, dc), device_id_type=pl.DeviceIdType.MESH
            )

    def blocks(w_ref, u):
        wide = [w_ref[u, v].astype(jnp.float32) for v in range(3)]
        nil = jnp.zeros((chan1, chan1), jnp.float32)
        upper = jnp.concatenate([wide[1], wide[0]], axis=0)
        lower = jnp.concatenate([wide[2], wide[1]], axis=0)
        after = jnp.concatenate([nil, wide[2]], axis=0)
        prior = jnp.concatenate([wide[0], nil], axis=0)
        return jnp.concatenate([part.T for part in (upper, lower, after, prior)], axis=0)

    depth = 4 * chan1
    for w_ref, t_ref in ((w1a_ref, t1a), (w1b_ref, t1b)):
        for u in range(3):
            t_ref[u * depth : (u + 1) * depth, :] = blocks(w_ref, u).astype(jnp.bfloat16)

    peers = sum(jnp.where(zero.exists(dr, dc), 1, 0) for dr, dc in zero.steps)
    pl.semaphore_wait(barrier, peers)
    zero.start(lambda dr, dc: True)

    for u in range(3):
        base = u * depth
        t2a[base : base + chan1, :] = w2a_ref[u, 1]
        t2a[base + chan1 : base + 2 * chan1, :] = w2a_ref[u, 2]
        t2a[base + 2 * chan1 : base + 3 * chan1, :] = jnp.zeros((chan1, chan2), jnp.bfloat16)
        t2a[base + 3 * chan1 : base + 4 * chan1, :] = w2a_ref[u, 0]
    for w_ref, t_ref in ((w2b_ref, t2b), (w3a_ref, t3a), (w3b_ref, t3b)):
        deep = w_ref.shape[3]
        for u in range(3):
            for v in range(3):
                flip = w_ref[u, v].astype(jnp.float32).T
                t_ref[(3 * u + v) * deep : (3 * u + v + 1) * deep, :] = flip.astype(jnp.bfloat16)
    stage[...] = jnp.zeros_like(stage)
    stage3[...] = jnp.zeros_like(stage3)
    stage4[...] = jnp.zeros_like(stage4)

    half = lax.broadcasted_iota(jnp.int32, (mid1, TILE), 1) < chan1
    half_own = lax.broadcasted_iota(jnp.int32, (pairs, TILE), 1) < chan1
    has_left, has_right = zero.exists(0, -1), zero.exists(0, 1)
    has_up, has_down = zero.exists(-1, 0), zero.exists(1, 0)
    ways = stage.shape[0]

    def at(i, size):
        return pl.ds(pl.multiple_of(i * size, 16), size)

    def load(halo, r, own_row):
        left = halo.left[r].astype(jnp.float32)
        right = halo.right[r].astype(jnp.float32)
        return left, own_row.astype(jnp.float32), right

    def spread(halo, r, own_row, way):
        left, row, right = load(halo, r, own_row)
        center = jnp.concatenate([left[8:16], row, right[0:8]], axis=0)
        stage[way, 8 : 8 + mid1, :] = center
        return center

    def fill1a(r, own_row, way):
        center = spread(zero, r, own_row, way)
        near = jnp.where(half, stage[way, 9 : 9 + mid1, :], stage[way, 7 : 7 + mid1, :])
        cat1a[at(r, mid1), :] = jnp.concatenate([center, near], axis=1).astype(jnp.bfloat16)

    def fill2a(r, target, own_row, way):
        center = spread(one, r, own_row, way)
        cat_row = jnp.concatenate([center, stage[way, 7 : 7 + mid1, :]], axis=1)
        target[at(r // 2, mid1), :] = cat_row.astype(jnp.bfloat16)

    def fill3a(r, target, own_row, way):
        left, row, right = load(two, r, own_row)
        stage3[way, 8 : 8 + SIDE, :] = left
        stage3[way, 8 + SIDE : 8 + SIDE + cols2, :] = row
        stage3[way, 8 + SIDE + cols2 : 8 + 2 * SIDE + cols2, :] = right
        parts = [stage3[way, pl.ds(7 + v, mid3, stride=2), :] for v in range(3)]
        target[at(r // 2, mid3), :] = jnp.concatenate(parts, axis=1).astype(jnp.bfloat16)

    def bias_of(at_row, times, width):
        return bias_ref[at_row : at_row + 1, 0:width] if times == 1 else None

    bias1a = jnp.concatenate([bias_ref[1:2, 0:chan1]] * 2, axis=1)
    bias1b = jnp.concatenate([bias_ref[1:2, chan1 : 2 * chan1]] * 2, axis=1)
    bias2a, bias2b = bias_ref[2:3, :], bias_ref[3:4, :]
    bias3a = jnp.concatenate([bias_ref[4:5, :], bias_ref[5:6, :]], axis=1)
    bias3b = jnp.concatenate([bias_ref[6:7, :], bias_ref[7:8, :]], axis=1)

    def masked(row, row_good):
        first = jnp.where(has_left & row_good, row[0:8], 0.0)
        last = jnp.where(has_right & row_good, row[row.shape[0] - 8 :], 0.0)
        inner = row[8 : row.shape[0] - 8]
        if row_good is not True:
            inner = jnp.where(row_good, inner, 0.0)
        return jnp.concatenate([first, inner, last], axis=0)

    def conv(lhs, weight, bias):
        total = jnp.dot(jnp.concatenate(lhs, axis=1), weight[...], preferred_element_type=jnp.float32)
        return jnp.maximum(total + bias, 0.0)

    def mid_one(i, count, good):
        lhs = [cat1a[pl.ds(pl.multiple_of((i + u) * mid1, 16), count * mid1), :] for u in range(3)]
        total = conv(lhs, t1a, bias1a)
        for k in range(count):
            row = masked(total[k * mid1 : (k + 1) * mid1], good)
            stage[k, 8 : 8 + mid1, :] = row
            near = jnp.where(half_own, stage[k, 17 : 17 + pairs, :], stage[k, 15 : 15 + pairs, :])
            cat_row = jnp.concatenate([row[8 : 8 + pairs], near], axis=1)
            cat1b[at(i + k, pairs), :] = cat_row.astype(jnp.bfloat16)

    def out_one(i, count):
        lhs = [cat1b[pl.ds(pl.multiple_of((i + u) * pairs, 16), count * pairs), :] for u in range(3)]
        total = conv(lhs, t1b, bias1b).astype(jnp.bfloat16)
        for k in range(count):
            one_ref[i + k] = total[k * pairs : (k + 1) * pairs]

    def mid_two(i, count, good):
        even = [cat2e[pl.ds((i + d) * mid1, count * mid1), :] for d in range(2)]
        odd = cat2o[pl.ds(i * mid1, count * mid1), :]
        total = conv([even[0], odd, even[1]], t2a, bias2a)
        for k in range(count):
            row = masked(total[k * mid1 : (k + 1) * mid1], good)
            stage[k % ways, 8 : 8 + mid1, :] = row
            down = stage[k % ways, 15 : 15 + cols2, :]
            up = stage[k % ways, 17 : 17 + cols2, :]
            cat_row = jnp.concatenate([down, row[8 : 8 + cols2], up], axis=1)
            cat2b[at(i + k, cols2), :] = cat_row.astype(jnp.bfloat16)

    def out_two(i, count):
        lhs = [cat2b[pl.ds((i + u) * cols2, count * cols2), :] for u in range(3)]
        total = conv(lhs, t2b, bias2b).astype(jnp.bfloat16)
        for k in range(count):
            two_ref[i + k] = total[k * cols2 : (k + 1) * cols2]

    def mid_three(i, count, good):
        even = [cat3e[pl.ds((i + d) * mid3, count * mid3), :] for d in range(2)]
        odd = cat3o[pl.ds(i * mid3, count * mid3), :]
        total = conv([even[0], odd, even[1]], t3a, bias3a)
        for k in range(count):
            row = masked(total[k * mid3 : (k + 1) * mid3], good)
            stage4[k % ways, 8 : 8 + mid3, :] = row
            down = stage4[k % ways, 15 : 15 + cols3, :]
            up = stage4[k % ways, 17 : 17 + cols3, :]
            cat_row = jnp.concatenate([down, row[8 : 8 + cols3], up], axis=1)
            cat3b[at(i + k, cols3), :] = cat_row.astype(jnp.bfloat16)

    zero.wait_recv(beside)

    def inner_fill(g, carry):
        for k in range(4):
            r = g * 4 + k
            fill1a(r + 2, bev_ref[r], k)
        return carry

    lax.fori_loop(0, rows1 // 4, inner_fill, 0)

    def inner_mid(g, carry):
        mid_one(2 + g * 2, 2, True)
        return carry

    lax.fori_loop(0, (rows1 - 2) // 2, inner_mid, 0)

    def inner_out(g, carry):
        out_one(2 + g * 2, 2)
        return carry

    lax.fori_loop(0, (rows1 - 4) // 2, inner_out, 0)
    zero.wait_recv(across)
    for k in range(2):
        fill1a(k, top0[k], k)
        fill1a(rows1 + 2 + k, bottom0[k], 2 + k)
    mid_one(0, 1, has_up)
    mid_one(1, 1, True)
    mid_one(rows1, 1, True)
    mid_one(rows1 + 1, 1, has_down)
    out_one(0, 2)
    out_one(rows1 - 2, 2)
    one.start(lambda dr, dc: True)

    one.wait_recv(beside)

    def inner_fill2(g, carry):
        for k in range(2):
            r = g * 4 + 2 * k
            fill2a(r + 3, cat2o, one_ref[r], 2 * k)
            fill2a(r + 4, cat2e, one_ref[r + 1], 2 * k + 1)
        return carry

    lax.fori_loop(0, rows1 // 4, inner_fill2, 0)
    for i in range(2, rows2, 2):
        mid_two(i, 2, True)
    mid_two(rows2, 1, True)
    for i in range(2, rows2 - 2, 2):
        out_two(i, 2)
    out_two(rows2 - 2, 1)
    one.wait_recv(across)
    fill2a(0, cat2e, top1[0], 0)
    fill2a(1, cat2o, top1[1], 1)
    fill2a(2, cat2e, top1[2], 2)
    fill2a(rows1 + 3, cat2o, bottom1[0], 3)
    fill2a(rows1 + 4, cat2e, bottom1[1], 0)
    mid_two(0, 1, has_up)
    mid_two(1, 1, True)
    mid_two(rows2 + 1, 1, has_down)
    out_two(0, 2)
    out_two(rows2 - 1, 1)
    two.start(lambda dr, dc: True)

    two.wait_recv(beside)
    for r in range(rows2):
        fill3a(r + 3, cat3o if r % 2 == 0 else cat3e, two_ref[r], r % ways)
    mid_three(2, rows3 - 1, True)
    two.wait_recv(across)
    fill3a(0, cat3e, top2[0], 0)
    fill3a(1, cat3o, top2[1], 1)
    fill3a(2, cat3e, top2[2], 2)
    fill3a(rows2 + 3, cat3o, bottom2[0], 3)
    fill3a(rows2 + 4, cat3e, bottom2[1], 0)
    mid_three(0, 1, has_up)
    mid_three(1, 1, True)
    mid_three(rows3 + 1, 1, has_down)
    lhs = [cat3b[u * cols3 : (u + rows3) * cols3, :] for u in range(3)]
    total = conv(lhs, t3b, bias3b).astype(jnp.bfloat16)
    three_ref[...] = total.reshape(rows3, cols3, chan3)
    for halo in (zero, one, two):
        halo.wait_send()


def levels(bev, convs, bias):
    rows1, pairs, _ = bev.shape
    w1a, w1b, w2a, w2b, w3a, w3b = convs
    chan1, chan2, chan3 = w1a.shape[2], w2b.shape[2], w3b.shape[2]
    rows2, rows3, cols2, cols3 = rows1 // 2, rows1 // 4, pairs, pairs // 2
    vmem = pl.BlockSpec(memory_space=pltpu.VMEM)
    mid1, mid3 = pairs + 16, cols3 + 16

    def buffers(rows, before, after):
        return [
            pltpu.VMEM((before, pairs, TILE), jnp.bfloat16),
            pltpu.VMEM((after, pairs, TILE), jnp.bfloat16),
            pltpu.VMEM((before + rows + after, SIDE, TILE), jnp.bfloat16),
            pltpu.VMEM((before + rows + after, SIDE, TILE), jnp.bfloat16),
        ]

    def half(*shape):
        return pltpu.VMEM(shape, jnp.bfloat16)

    return pl.pallas_call(
        levels_kernel,
        in_specs=[vmem] * 8,
        out_specs=[vmem] * 3,
        out_shape=[
            jax.ShapeDtypeStruct((rows1, pairs, TILE), jnp.bfloat16),
            jax.ShapeDtypeStruct((rows2, cols2, chan2), jnp.bfloat16),
            jax.ShapeDtypeStruct((rows3, cols3, chan3), jnp.bfloat16),
        ],
        scratch_shapes=buffers(rows1, 2, 2)
        + buffers(rows1, 3, 2)
        + buffers(rows2, 3, 2)
        + [pltpu.SemaphoreType.DMA((3, len(STEPS)))] * 2
        + [
            half(12 * chan1, 2 * chan1),
            half(12 * chan1, 2 * chan1),
            half(12 * chan1, chan2),
            half(9 * chan2, chan2),
            half(9 * chan2, chan3),
            half(9 * chan3, chan3),
            half((rows1 + 4) * mid1, 4 * chan1),
            half((rows1 + 2) * pairs, 4 * chan1),
            half((rows2 + 3) * mid1, 4 * chan1),
            half((rows2 + 2) * mid1, 4 * chan1),
            half((rows2 + 2) * cols2, 3 * chan2),
            half((rows3 + 3) * mid3, 3 * chan2),
            half((rows3 + 2) * mid3, 3 * chan2),
            half((rows3 + 2) * cols3, 3 * chan3),
            pltpu.VMEM((4, mid1 + 16, TILE), jnp.float32),
            pltpu.VMEM((4, cols2 + 2 * SIDE + 16, TILE), jnp.float32),
            pltpu.VMEM((4, mid3 + 16, chan3), jnp.float32),
        ],
        compiler_params=pltpu.CompilerParams(collective_id=8, has_side_effects=True),
        name="levels",
    )(bev, *convs, bias)


def lift_kernel(
    one_ref, two_ref, three_ref, near_ref, mid_ref, far_ref, bias_ref, out_ref,
    result, expand1, expand2, expand3, gather, sem,
):
    rows, pairs, _ = one_ref.shape
    up = near_ref.shape[1]
    cols = 2 * pairs
    near = near_ref[...].astype(jnp.float32)
    near = jnp.concatenate([near, near], axis=0).T.astype(jnp.bfloat16)
    expand2[...] = jnp.zeros_like(expand2)
    expand3[...] = jnp.zeros_like(expand3)
    first_half = lax.broadcasted_iota(jnp.int32, (pairs, TILE), 1) < TILE // 2

    def product(weight, wide):
        return lax.dot_general(
            weight, wide, (((1,), (1,)), ((), ())), preferred_element_type=jnp.float32
        )

    def put(row, value, bias):
        for h in range(cols // TILE):
            piece = jnp.maximum(value[:, h * TILE : (h + 1) * TILE] + bias, 0.0)
            gather[h, pl.ds(row, up, stride=rows), :] = piece

    def finish(which):
        for h in range(cols // TILE):
            done = gather[h].astype(jnp.bfloat16).reshape(up, rows, TILE)
            result[which, :, :, h * TILE : (h + 1) * TILE] = done
        pltpu.make_async_copy(
            result.at[which], out_ref.at[pl.ds(which * up, up)], sem.at[which]
        ).start()

    def bias_tile(at_row):
        return jnp.broadcast_to(bias_ref[at_row : at_row + 1, :], (TILE, up)).T

    bias = bias_tile(8)
    for r in range(rows):
        row = one_ref[r].astype(jnp.float32)
        way = r % 2
        expand1[way, pl.ds(0, pairs, stride=2), :] = jnp.where(first_half, row, 0.0)
        expand1[way, pl.ds(1, pairs, stride=2), :] = jnp.where(first_half, 0.0, row)
        put(r, product(near, expand1[way].astype(jnp.bfloat16)), bias)
    finish(0)

    bias = bias_tile(9)
    factor = mid_ref.shape[0]
    weight = [
        jnp.concatenate([mid_ref[a, e] for e in range(factor)], axis=1) for a in range(factor)
    ]
    weight = jnp.concatenate(weight, axis=0)
    for i in range(two_ref.shape[0]):
        row = two_ref[i].astype(jnp.float32)
        way = i % 2
        for e in range(factor):
            expand2[way, e, pl.ds(e, row.shape[0], stride=factor), :] = row
        wide = jnp.concatenate([expand2[way, e] for e in range(factor)], axis=1)
        total = product(weight, wide.astype(jnp.bfloat16))
        for a in range(factor):
            put(i * factor + a, total[a * up : (a + 1) * up], bias)
    finish(1)

    bias = bias_tile(10)
    factor = far_ref.shape[0]
    weight = [
        jnp.concatenate([far_ref[a, e] for e in range(factor)], axis=1) for a in range(factor)
    ]
    weight = jnp.concatenate(weight, axis=0)
    halves = three_ref.shape[2] // TILE
    for i in range(three_ref.shape[0]):
        row = three_ref[i].astype(jnp.float32)
        for e in range(factor):
            for h in range(halves):
                expand3[e * halves + h, pl.ds(e, row.shape[0], stride=factor), :] = row[
                    :, h * TILE : (h + 1) * TILE
                ]
        wide = jnp.concatenate([expand3[k] for k in range(factor * halves)], axis=1)
        total = product(weight, wide.astype(jnp.bfloat16))
        for a in range(factor):
            put(i * factor + a, total[a * up : (a + 1) * up], bias)
    finish(2)
    for which in range(3):
        pltpu.make_async_copy(
            result.at[which], out_ref.at[pl.ds(which * up, up)], sem.at[which]
        ).wait()


def lifts(maps, weights, bias):
    rows, pairs, _ = maps[0].shape
    near, mid, far = weights
    up = near.shape[1]
    cols = 2 * pairs
    vmem = pl.BlockSpec(memory_space=pltpu.VMEM)
    factor, halves = far.shape[0], far.shape[3] // TILE
    return pl.pallas_call(
        lift_kernel,
        in_specs=[vmem] * 7,
        out_specs=pl.BlockSpec(memory_space=pl.ANY),
        out_shape=jax.ShapeDtypeStruct((3 * up, rows, cols), jnp.bfloat16),
        scratch_shapes=[
            pltpu.VMEM((3, up, rows, cols), jnp.bfloat16),
            pltpu.VMEM((2, cols, TILE), jnp.float32),
            pltpu.VMEM((2, mid.shape[0], cols, TILE), jnp.float32),
            pltpu.VMEM((factor * halves, cols, TILE), jnp.float32),
            pltpu.VMEM((cols // TILE, up * rows, TILE), jnp.float32),
            pltpu.SemaphoreType.DMA((3,)),
        ],
        name="lifts",
    )(*maps, near, mid, far, bias)


def on_device(
    points,
    pillar_cell,
    point_count,
    tile_count,
    point_embed,
    point_mix,
    first_conv,
    second_conv,
    third_conv,
    fourth_conv,
    fifth_conv,
    sixth_conv,
    near_lift,
    mid_lift,
    far_lift,
    biases,
):
    tile_num = tile_count.shape[0]
    capacity = points.shape[2] // tile_num
    bias = biases.reshape(-1, TILE)
    vectors, places = encode_all(
        points,
        point_count.reshape(tile_num, 1, capacity),
        pillar_cell.reshape(tile_num, 1, capacity),
        tile_count,
        jnp.transpose(point_embed),
        point_mix,
        bias,
    )
    chan = point_mix.shape[0]
    bev = scatter_max(places.reshape(-1), vectors)
    bev = bev.reshape(ROWS_DEV, COLS_DEV // 2, 2 * chan)
    convs = (
        first_conv,
        second_conv,
        jnp.transpose(third_conv, (0, 1, 3, 2)),
        fourth_conv,
        fifth_conv,
        sixth_conv,
    )
    maps = levels(bev, convs, bias)
    near = jnp.transpose(near_lift, (0, 1, 3, 2)).reshape(near_lift.shape[3], near_lift.shape[2])
    return lifts(maps, (near, mid_lift, far_lift), bias)


def solution(mesh):
    return jax.shard_map(
        on_device,
        mesh=mesh,
        in_specs=(
            P(None, None, ("slab", "row", "col")),
            P(("slab", "row", "col")),
            P(("slab", "row", "col")),
            P(("slab", "row", "col")),
            P(),
            P(),
            P(),
            P(),
            P(),
            P(),
            P(),
            P(),
            P(),
            P(),
            P(),
            P(),
        ),
        out_specs=P(None, ("slab", "row"), "col"),
        check_vma=False,
    )
```

time: 105 us -> 68.1 us (0.65)
  Pallas kernels: 86.4 us -> 67.7 us
  local copies, waits for them, and re-layouts: 9.85 us -> 0 us
  matrix products: 4.21 us -> 0 us
  other arithmetic: 3.63 us -> 0 us
    pallas_call x8 -> x3, Pallas kernels: 76.4 us -> 54.2 us  [the longest x1 24.9 us: levels(): pl.pallas_call(levels_kernel, in_specs=[vmem] * 8, out_specs=[vmem] * 3,...]
    unnamed x16 -> x0, local copies, waits for them, and re-layouts: 4.31 us -> none
    dot_general x3 -> x0, matrix products: 4.21 us -> none  [lift_layer(): jnp.einsum('oak,ijk->oiaj', weight, wide, preferred_element_type=jnp.floa...]
    pallas_call x1, Pallas kernels: 10 us -> 13.5 us  [scatter_max(): pl.pallas_call(scatter_kernel, in_specs=[pl.BlockSpec(memory_space=pltpu....]
    concatenate x1 -> x0, local copies, waits for them, and re-layouts: 3.44 us -> none  [on_device(): return jnp.concatenate([near, middle, distant], axis=0)]
    select_n x1 -> x0, other arithmetic: 1.4 us -> none  [on_device(): jnp.where(live_slot, point_count.reshape(tile_num, capacity), 0)]
    add x1 -> x0, other arithmetic: 1.34 us -> none  [on_device(): local_cell = row_local * COLS_DEV + pillar_cell % COLS_DEV]
    reshape x1 -> x0, local copies, waits for them, and re-layouts: 1.3 us -> none  [on_device(): lead = biases.reshape(1, -1)]
where the time goes in v1:
time: 68.1 us; the launch traced here: 67.8 us
  Pallas kernels  67.7 us (99%)
    pallas_call x1, Pallas kernels, levels(): pl.pallas_call(levels_kernel, in_specs=[vmem] * 8, out_specs=[vmem] * 3,...  24.9 us
    pallas_call x1, Pallas kernels, encode_all(): pl.pallas_call(encode_kernel, in_specs=[vmem] * 6 + [pl.BlockSpec(memory_...  22.6 us
    pallas_call x1, Pallas kernels, scatter_max(): pl.pallas_call(scatter_kernel, in_specs=[pl.BlockSpec(memory_space=pltpu....  13.5 us
    pallas_call x1, Pallas kernels, lifts(): pl.pallas_call(lift_kernel, in_specs=[vmem] * 7, out_specs=pl.BlockSpec(m...  6.74 us

profile of v1, /device:TPU:9, one launch (start us, length us, event | category | flops | bytes accessed | tf_op | source)
XLA Modules:
  0.0 67.8 jit_solution(10075550657598804286)
XLA Ops:
  0.0 22.6 %encode_send.1 = (bf16[16,64,256]{2,1,0:T(8,128)(2,1)}, s32[16,1,256]{2,1,0:T(1,128)}) custom-call(bf16[9,32,4096]{2,1,0:T(8,128)(2,1)} %x_ref.1, s32[16,1,256]{2,1,0:T(1,128)} %bitcast.15, s32[16,1,256]{2,1,0:T(1,128)} %bitcast.16, bf16[9,64]{1,0:T(8,128)(2,1)} %bitcast.19, bf16[64,64]{1,0:T(8,128)(2,1)} %mix_ref.1, f32[11,128]{1,0:T(8,128)} %bitcast.12, ...), custom_call_target="tpu_custom_call" | custom-call | tf_op jit(solution)/shard_map/encode_send/pallas_call | solution.py:137
  22.6 13.5 %scatter_max.1 = bf16[2048,128]{1,0:T(8,128)(2,1)} custom-call(s32[4096]{0:T(1024)} %bitcast.18, bf16[16,64,256]{2,1,0:T(8,128)(2,1)} %get-tuple-element.11.vec_ref), custom_call_target="tpu_custom_call" | custom-call | tf_op jit(solution)/shard_map/scatter_max/pallas_call | solution.py:202
  36.1 24.9 %levels.1 = (bf16[16,128,128]{2,1,0:T(8,128)(2,1)}, bf16[8,128,128]{2,1,0:T(8,128)(2,1)}, bf16[4,64,256]{2,1,0:T(8,128)(2,1)}) custom-call(bf16[16,128,128]{2,1,0:T(8,128)(2,1)} %bitcast.10, bf16[3,3,64,64]{3,2,1,0:T(8,128)(2,1)} %w1a_ref.1, bf16[3,3,64,64]{3,2,1,0:T(8,128)(2,1)} %w1b_ref.1, bf16[3,3,64,128]{3,2,1,0:T(8,128)(2,1)} %bitcast.11, ...), custom_call_target="tpu_custom_call" | custom-call | tf_op jit(solution)/shard_map/levels/pallas_call | solution.py:562
  60.9 6.7 %lifts.1 = bf16[384,16,256]{2,1,0:T(8,128)(2,1)} custom-call(bf16[16,128,128]{2,1,0:T(8,128)(2,1)} %get-tuple-element.12.one_ref, bf16[8,128,128]{2,1,0:T(8,128)(2,1)} %get-tuple-element.13.two_ref, bf16[4,64,256]{2,1,0:T(8,128)(2,1)} %get-tuple-element.14.three_ref, bf16[64,128]{1,0:T(8,128)(2,1)} %bitcast.17, bf16[2,2,128,128]{3,2,1,0:T(8,128)(2,1)} %mid_ref.1, ...), custom_call_target="tpu_custom_call" | custom-call | tf_op jit(solution)/shard_map/lifts/pallas_call | solution.py:691

commit v2 on v1

--- a/solution.py
+++ b/solution.py
@@ -161,44 +161,55 @@
 
 def scatter_kernel(cell_ref, vec_ref, out_ref, stage, *grids):
     tiles, chan, cap = vec_ref.shape
-    area = out_ref.shape[0]
-    for grid in grids:
-        grid[...] = jnp.zeros_like(grid)
-    lanes = len(grids)
-    first_half = lax.broadcasted_iota(jnp.int32, (cap, 2 * chan), 1) < chan
-
-    def per_tile(t, carry):
+    pairs = out_ref.shape[0]
+    share = 2 * pairs // tiles
+
+    def prepare(t, carry):
         twice = vec_ref[t].astype(jnp.float32)
         twice = jnp.concatenate([twice, twice], axis=0).T
-        stage[0:cap, :] = jnp.where(first_half, twice, 0.0)
-        stage[cap : 2 * cap, :] = jnp.where(first_half, 0.0, twice)
-        unroll = 32 // lanes
-
-        def per_slot(s, inner):
-            for k in range(unroll):
-                base = (s * unroll + k) * lanes
-                cells = [cell_ref[t * cap + base + a] for a in range(lanes)]
-                pairs = [lax.shift_right_logical(cell, 1) for cell in cells]
-                rows = [base + a + (cells[a] & 1) * cap for a in range(lanes)]
-                olds = [grids[a][pl.ds(pairs[a], 1), :] for a in range(lanes)]
-                for a in range(lanes):
-                    grids[a][pl.ds(pairs[a], 1), :] = jnp.maximum(
-                        olds[a], stage[pl.ds(rows[a], 1), :]
-                    )
-            return inner
-
-        return lax.fori_loop(0, cap // (lanes * unroll), per_slot, carry)
-
-    lax.fori_loop(0, tiles, per_tile, 0)
-    total = grids[0][...]
-    for grid in grids[1:]:
-        total = jnp.maximum(total, grid[...])
-    out_ref[...] = total.astype(jnp.bfloat16)
+        stage[pl.ds(pl.multiple_of(t * cap, cap), cap), :] = twice
+        for grid in grids:
+            grid[pl.ds(pl.multiple_of(t * share, share), share), :] = jnp.zeros(
+                (share, 2 * chan), jnp.float32
+            )
+        return carry
+
+    lax.fori_loop(0, tiles, prepare, 0, unroll=2)
+    lanes = len(grids)
+    batch = 32
+
+    def scatter(s, carry):
+        start = s * batch
+        for k in range(0, batch, lanes):
+            cells = [cell_ref[start + (k + a)] for a in range(lanes)]
+            olds = [grids[a][pl.ds(cells[a], 1), :] for a in range(lanes)]
+            news = [stage[pl.ds(start + (k + a), 1), :] for a in range(lanes)]
+            for a in range(lanes):
+                grids[a][pl.ds(cells[a], 1), :] = jnp.maximum(olds[a], news[a])
+        return carry
+
+    lax.fori_loop(0, tiles * cap // batch, scatter, 0)
+    part = min(pairs, 256)
+    first_half = lax.broadcasted_iota(jnp.int32, (part, 2 * chan), 1) < chan
+
+    def finish(i, carry):
+        base = pl.multiple_of(i * 2 * part, 2 * part)
+        sides = []
+        for side in range(2):
+            total = grids[0][pl.ds(base + side, part, stride=2), :]
+            for grid in grids[1:]:
+                total = jnp.maximum(total, grid[pl.ds(base + side, part, stride=2), :])
+            sides.append(total)
+        total = jnp.where(first_half, sides[0], sides[1])
+        out_ref[pl.ds(pl.multiple_of(i * part, part), part), :] = total.astype(jnp.bfloat16)
+        return carry
+
+    lax.fori_loop(0, pairs // part, finish, 0)
 
 
 def scatter_max(cells, vectors):
     tiles, chan, cap = vectors.shape
-    area = ROWS_DEV * COLS_DEV // 2
+    area = ROWS_DEV * COLS_DEV
     return pl.pallas_call(
         scatter_kernel,
         in_specs=[
@@ -206,8 +217,8 @@
             pl.BlockSpec(memory_space=pltpu.VMEM),
         ],
         out_specs=pl.BlockSpec(memory_space=pltpu.VMEM),
-        out_shape=jax.ShapeDtypeStruct((area, 2 * chan), jnp.bfloat16),
-        scratch_shapes=[pltpu.VMEM((2 * cap, 2 * chan), jnp.float32)]
+        out_shape=jax.ShapeDtypeStruct((area // 2, 2 * chan), jnp.bfloat16),
+        scratch_shapes=[pltpu.VMEM((tiles * cap, 2 * chan), jnp.float32)]
         + [pltpu.VMEM((area, 2 * chan), jnp.float32)] * LANES,
         name="scatter_max",
     )(cells, vectors)

time: 68.1 us -> 63.1 us (0.927)
  Pallas kernels: 67.7 us -> 62.7 us
    pallas_call x1, Pallas kernels: 13.5 us -> 8.5 us  [scatter_max(): pl.pallas_call(scatter_kernel, in_specs=[pl.BlockSpec(memory_space=pltpu....]
where the time goes in v2:
time: 63.1 us; the launch traced here: 62.9 us
  Pallas kernels  62.7 us (99%)
    pallas_call x1, Pallas kernels, levels(): pl.pallas_call(levels_kernel, in_specs=[vmem] * 8, out_specs=[vmem] * 3,...  24.9 us
    pallas_call x1, Pallas kernels, encode_all(): pl.pallas_call(encode_kernel, in_specs=[vmem] * 6 + [pl.BlockSpec(memory_...  22.6 us
    pallas_call x1, Pallas kernels, scatter_max(): pl.pallas_call(scatter_kernel, in_specs=[pl.BlockSpec(memory_space=pltpu....  8.5 us
    pallas_call x1, Pallas kernels, lifts(): pl.pallas_call(lift_kernel, in_specs=[vmem] * 7, out_specs=pl.BlockSpec(m...  6.74 us

profile of v2, /device:TPU:9, one launch (start us, length us, event | category | flops | bytes accessed | tf_op | source)
XLA Modules:
  0.0 62.9 jit_solution(18294189768145249647)
XLA Ops:
  0.0 22.6 %encode_send.1 = (bf16[16,64,256]{2,1,0:T(8,128)(2,1)}, s32[16,1,256]{2,1,0:T(1,128)}) custom-call(bf16[9,32,4096]{2,1,0:T(8,128)(2,1)} %x_ref.1, s32[16,1,256]{2,1,0:T(1,128)} %bitcast.15, s32[16,1,256]{2,1,0:T(1,128)} %bitcast.16, bf16[9,64]{1,0:T(8,128)(2,1)} %bitcast.19, bf16[64,64]{1,0:T(8,128)(2,1)} %mix_ref.1, f32[11,128]{1,0:T(8,128)} %bitcast.12, ...), custom_call_target="tpu_custom_call" | custom-call | tf_op jit(solution)/shard_map/encode_send/pallas_call | solution.py:137
  22.6 8.5 %scatter_max.1 = bf16[2048,128]{1,0:T(8,128)(2,1)} custom-call(s32[4096]{0:T(1024)} %bitcast.18, bf16[16,64,256]{2,1,0:T(8,128)(2,1)} %get-tuple-element.11.vec_ref), custom_call_target="tpu_custom_call" | custom-call | tf_op jit(solution)/shard_map/scatter_max/pallas_call | solution.py:213
  31.1 24.9 %levels.1 = (bf16[16,128,128]{2,1,0:T(8,128)(2,1)}, bf16[8,128,128]{2,1,0:T(8,128)(2,1)}, bf16[4,64,256]{2,1,0:T(8,128)(2,1)}) custom-call(bf16[16,128,128]{2,1,0:T(8,128)(2,1)} %bitcast.10, bf16[3,3,64,64]{3,2,1,0:T(8,128)(2,1)} %w1a_ref.1, bf16[3,3,64,64]{3,2,1,0:T(8,128)(2,1)} %w1b_ref.1, bf16[3,3,64,128]{3,2,1,0:T(8,128)(2,1)} %bitcast.11, ...), custom_call_target="tpu_custom_call" | custom-call | tf_op jit(solution)/shard_map/levels/pallas_call | solution.py:573
  56.0 6.7 %lifts.1 = bf16[384,16,256]{2,1,0:T(8,128)(2,1)} custom-call(bf16[16,128,128]{2,1,0:T(8,128)(2,1)} %get-tuple-element.12.one_ref, bf16[8,128,128]{2,1,0:T(8,128)(2,1)} %get-tuple-element.13.two_ref, bf16[4,64,256]{2,1,0:T(8,128)(2,1)} %get-tuple-element.14.three_ref, bf16[64,128]{1,0:T(8,128)(2,1)} %bitcast.17, bf16[2,2,128,128]{3,2,1,0:T(8,128)(2,1)} %mid_ref.1, ...), custom_call_target="tpu_custom_call" | custom-call | tf_op jit(solution)/shard_map/lifts/pallas_call | solution.py:702

commit v3 on v2

--- a/solution.py
+++ b/solution.py
@@ -16,7 +16,8 @@
 
 def encode_kernel(
     x_ref, count_ref, cell_ref, embed_ref, mix_ref, bias_ref, live_ref, out_ref, place_ref,
-    send_ref, place_send, w1_ref, w2_ref, b1_ref, b2_ref, ssem, rsem, place_ssem, place_rsem
+    x_tiles, send_ref, place_send, w1_ref, w2_ref, b1_ref, b2_ref, x_sem, ssem, rsem,
+    place_ssem, place_rsem
 ):
     feat, points, _ = x_ref.shape
     tiles, _, cap = count_ref.shape
@@ -25,9 +26,31 @@
     col_count = lax.axis_size("col")
     me = lax.axis_index("row") * col_count + lax.axis_index("col")
 
+    side, rank = me // half, me % half
+
     def device_of(tile):
         return {"row": tile // col_count, "col": tile % col_count}
 
+    def tile_of(k):
+        own = k // half
+        return (side + 1 + own) % 2 * half + (rank + k + own) % half
+
+    def source_of(k):
+        own = k // half
+        return (side + 1 + own) % 2 * half + (rank - k - own + 2 * half) % half
+
+    def fetch(tile):
+        start = pl.multiple_of(tile * cap, cap)
+        return pltpu.make_async_copy(
+            x_ref.at[:, :, pl.ds(start, cap)], x_tiles.at[tile], x_sem.at[tile]
+        )
+
+    def fetch_start(k, carry):
+        fetch(tile_of(k)).start()
+        return carry
+
+    lax.fori_loop(0, tiles - 1, fetch_start, 0)
+    fetch(me).start()
     barrier = pltpu.get_barrier_semaphore()
 
     def greet(i, carry):
@@ -68,10 +91,10 @@
     def encode(tile, dest_ref):
         slot = lax.broadcasted_iota(jnp.int32, (1, cap), 1)
         count = jnp.where(slot < live_ref[tile], count_ref[tile], 0)
-        start = pl.multiple_of(tile * cap, cap)
+        fetch(tile).wait()
         best = jnp.full((chan, cap), -jnp.inf, jnp.float32)
         for h in range(points // HALF):
-            block = x_ref[:, h * HALF : (h + 1) * HALF, pl.ds(start, cap)]
+            block = x_tiles[tile, :, h * HALF : (h + 1) * HALF, :]
             block = block.reshape(feat * HALF, cap)
             for q in range(HALF // PACK):
                 hidden = jnp.dot(w1_ref[q], block, preferred_element_type=jnp.float32)
@@ -84,65 +107,61 @@
         vec = jnp.maximum(best + b2_ref[...], 0.0)
         dest_ref[tile] = vec.astype(jnp.bfloat16)
 
-    def place_of(i, slot):
-        tile = (me + i) % tiles
+    def copy_of(k, source, target, send_sem, recv_sem):
         return pltpu.make_async_remote_copy(
-            src_ref=place_send.at[tile],
-            dst_ref=place_ref.at[slot],
-            send_sem=place_ssem.at[i],
-            recv_sem=place_rsem.at[i],
-            device_id=device_of(tile),
+            src_ref=source.at[tile_of(k)],
+            dst_ref=target,
+            send_sem=send_sem.at[k],
+            recv_sem=recv_sem.at[k],
+            device_id=device_of(tile_of(k)),
             device_id_type=pl.DeviceIdType.MESH,
         )
 
-    def copy_of(i, slot):
-        tile = (me + i) % tiles
-        return pltpu.make_async_remote_copy(
-            src_ref=send_ref.at[tile],
-            dst_ref=out_ref.at[slot],
-            send_sem=ssem.at[i],
-            recv_sem=rsem.at[i],
-            device_id=device_of(tile),
-            device_id_type=pl.DeviceIdType.MESH,
-        )
+    def copies(k, slot):
+        return [
+            copy_of(k, send_ref, out_ref.at[slot], ssem, rsem),
+            copy_of(k, place_send, place_ref.at[slot], place_ssem, place_rsem),
+        ]
 
     pl.semaphore_wait(barrier, tiles - 1)
 
     def step(k, carry):
-        i = half + (1 - 2 * (k % 2)) * ((k + 1) // 2)
-        encode((me + i) % tiles, send_ref)
-        copy_of(i, me).start()
-        place_of(i, me).start()
+        encode(tile_of(k), send_ref)
+        for copy in copies(k, me):
+            copy.start()
         return carry
 
     lax.fori_loop(0, tiles - 1, step, 0, unroll=3)
     encode(me, out_ref)
     place_ref[me] = place_send[me]
 
-    def finish(i, carry):
-        copy_of(i, me).wait_send()
-        place_of(i, me).wait_send()
-        copy_of(i, (me - i + tiles) % tiles).wait_recv()
-        place_of(i, (me - i + tiles) % tiles).wait_recv()
-        return carry
-
-    lax.fori_loop(1, tiles, finish, 0)
+    def finish(k, carry):
+        for copy in copies(k, me):
+            copy.wait_send()
+        for copy in copies(k, source_of(k)):
+            copy.wait_recv()
+        return carry
+
+    lax.fori_loop(0, tiles - 1, finish, 0)
 
 
 def encode_all(points, counts, cells, live, embed, mix, bias):
-    feat = points.shape[0]
+    feat, depth, _ = points.shape
     tiles, _, cap = counts.shape
     chan, mid = mix.shape
     vmem = pl.BlockSpec(memory_space=pltpu.VMEM)
     return pl.pallas_call(
         encode_kernel,
-        in_specs=[vmem] * 6 + [pl.BlockSpec(memory_space=pltpu.SMEM)],
+        in_specs=[pl.BlockSpec(memory_space=pl.ANY)]
+        + [vmem] * 5
+        + [pl.BlockSpec(memory_space=pltpu.SMEM)],
         out_specs=[vmem, vmem],
         out_shape=[
             jax.ShapeDtypeStruct((tiles, chan, cap), jnp.bfloat16),
             jax.ShapeDtypeStruct((tiles, 1, cap), jnp.int32),
         ],
         scratch_shapes=[
+            pltpu.VMEM((tiles, feat, depth, cap), jnp.bfloat16),
             pltpu.VMEM((tiles, chan, cap), jnp.bfloat16),
             pltpu.VMEM((tiles, 1, cap), jnp.int32),
             pltpu.VMEM((HALF // PACK, PACK * mid, feat * HALF), jnp.bfloat16),
@@ -153,6 +172,7 @@
             pltpu.SemaphoreType.DMA((tiles,)),
             pltpu.SemaphoreType.DMA((tiles,)),
             pltpu.SemaphoreType.DMA((tiles,)),
+            pltpu.SemaphoreType.DMA((tiles,)),
         ],
         compiler_params=pltpu.CompilerParams(collective_id=7, has_side_effects=True),
         name="encode_send",
@@ -176,7 +196,7 @@
 
     lax.fori_loop(0, tiles, prepare, 0, unroll=2)
     lanes = len(grids)
-    batch = 32
+    batch = 64
 
     def scatter(s, carry):
         start = s * batch
@@ -302,21 +322,144 @@
     return dr == 0
 
 
+def product(weight, wide_row):
+    return lax.dot_general(
+        weight, wide_row, (((1,), (1,)), ((), ())), preferred_element_type=jnp.float32
+    )
+
+
+def put_row(gather, rows, row, value, bias):
+    for h in range(gather.shape[0]):
+        piece = jnp.maximum(value[:, h * TILE : (h + 1) * TILE] + bias, 0.0)
+        gather[h, pl.ds(row, value.shape[0], stride=rows), :] = piece
+
+
+def take_rows(gather, rows, target):
+    for h in range(gather.shape[0]):
+        done = gather[h].astype(jnp.bfloat16).reshape(-1, rows, TILE)
+        target[:, :, h * TILE : (h + 1) * TILE] = done
+
+
+def stacked(w_ref):
+    factor = w_ref.shape[0]
+    weight = [jnp.concatenate([w_ref[a, e] for e in range(factor)], axis=1) for a in range(factor)]
+    return jnp.concatenate(weight, axis=0)
+
+
+def far_kernel(
+    upper_hbm, three_hbm, far_hbm, bias_hbm, out_ref,
+    upper, three_ref, far_ref, bias_ref, result, expand, gather, load_sem, out_sem,
+):
+    up, rows, _ = result.shape
+    pieces = upper.shape[0] // up
+    loads = [
+        pltpu.make_async_copy(source, target, load_sem.at[place])
+        for place, (source, target) in enumerate(
+            [(three_hbm, three_ref), (bias_hbm, bias_ref), (far_hbm, far_ref)]
+        )
+    ]
+    passing = [
+        (
+            pltpu.make_async_copy(
+                upper_hbm.at[pl.ds(k * up, up)], upper.at[pl.ds(k * up, up)], load_sem.at[3 + k]
+            ),
+            pltpu.make_async_copy(
+                upper.at[pl.ds(k * up, up)], out_ref.at[pl.ds(k * up, up)], out_sem.at[k]
+            ),
+        )
+        for k in range(pieces)
+    ]
+    for copy in loads:
+        copy.start()
+    for copy_in, _ in passing:
+        copy_in.start()
+    expand[...] = jnp.zeros_like(expand)
+    for copy in loads:
+        copy.wait()
+    last = bias_ref.shape[0] - 1
+    bias = jnp.broadcast_to(bias_ref[last : last + 1, :], (TILE, up)).T
+    factor = far_ref.shape[0]
+    rows3, cols3, chan3 = three_ref.shape
+    weight = stacked(far_ref)
+    halves = chan3 // TILE
+    for i in range(rows3):
+        row = three_ref[i].astype(jnp.float32)
+        for e in range(factor):
+            for h in range(halves):
+                piece = row[:, h * TILE : (h + 1) * TILE]
+                expand[e * halves + h, pl.ds(e, cols3, stride=factor), :] = piece
+        wide_row = jnp.concatenate([expand[k] for k in range(factor * halves)], axis=1)
+        total = product(weight, wide_row.astype(jnp.bfloat16))
+        for a in range(factor):
+            put_row(gather, rows, i * factor + a, total[a * up : (a + 1) * up], bias)
+        if i < pieces:
+            passing[i][0].wait()
+            passing[i][1].start()
+    take_rows(gather, rows, result)
+    final = pltpu.make_async_copy(result, out_ref.at[pl.ds(pieces * up, up)], out_sem.at[pieces])
+    final.start()
+    for _, copy_out in passing:
+        copy_out.wait()
+    final.wait()
+
+
+def far_lift_all(upper, three, far, bias):
+    up = far.shape[2]
+    two_up, rows, cols = upper.shape
+    operands = (upper, three, far, bias)
+    return pl.pallas_call(
+        far_kernel,
+        in_specs=[pl.BlockSpec(memory_space=pl.ANY)] * len(operands),
+        out_specs=pl.BlockSpec(memory_space=pl.ANY),
+        out_shape=jax.ShapeDtypeStruct((two_up + up, rows, cols), jnp.bfloat16),
+        scratch_shapes=[pltpu.VMEM(operand.shape, operand.dtype) for operand in operands]
+        + [
+            pltpu.VMEM((up, rows, cols), jnp.bfloat16),
+            pltpu.VMEM((far.shape[0] * far.shape[3] // TILE, cols, TILE), jnp.float32),
+            pltpu.VMEM((cols // TILE, up * rows, TILE), jnp.float32),
+            pltpu.SemaphoreType.DMA((3 + two_up // up,)),
+            pltpu.SemaphoreType.DMA((1 + two_up // up,)),
+        ],
+        name="far_lift",
+    )(*operands)
+
+
 def levels_kernel(
-    bev_ref, w1a_ref, w1b_ref, w2a_ref, w2b_ref, w3a_ref, w3b_ref, bias_ref,
-    one_ref, two_ref, three_ref,
+    bev_hbm, w1a_hbm, w1b_hbm, w2a_hbm, w2b_hbm, w3a_hbm, w3b_hbm, near_hbm, mid_hbm, bias_hbm,
+    out_ref, three_hbm,
+    bev_ref, w1a_ref, w1b_ref, w2a_ref, w2b_ref, w3a_ref, w3b_ref, near_ref, mid_ref, bias_ref,
+    load_sem, one_ref, two_ref, three_ref,
     top0, bottom0, left0, right0, top1, bottom1, left1, right1, top2, bottom2, left2, right2,
     send_sem, recv_sem,
     t1a, t1b, t2a, t2b, t3a, t3b, cat1a, cat1b, cat2e, cat2o, cat2b, cat3e, cat3o, cat3b,
-    stage, stage3, stage4,
+    stage, stage3, stage4, result, expand1, expand2, gather, out_sem,
 ):
+    loads = [
+        pltpu.make_async_copy(source, target, load_sem.at[place])
+        for place, (source, target) in enumerate(
+            [
+                (bev_hbm, bev_ref),
+                (bias_hbm, bias_ref),
+                (w1a_hbm, w1a_ref),
+                (w1b_hbm, w1b_ref),
+                (w2a_hbm, w2a_ref),
+                (w2b_hbm, w2b_ref),
+                (w3a_hbm, w3a_ref),
+                (w3b_hbm, w3b_ref),
+                (near_hbm, near_ref),
+                (mid_hbm, mid_ref),
+            ]
+        )
+    ]
+    for copy in loads:
+        copy.start()
     rows1, pairs, _ = bev_ref.shape
     rows2, cols2, chan2 = two_ref.shape
     rows3, cols3, chan3 = three_ref.shape
     chan1 = w1a_ref.shape[2]
     mid1 = pairs + 16
     mid3 = cols3 + 16
-    zero = Halo(0, bev_ref, top0, bottom0, left0, right0, send_sem, recv_sem)
+    zero = Halo(0, bev_hbm, top0, bottom0, left0, right0, send_sem, recv_sem)
     one = Halo(1, one_ref, top1, bottom1, left1, right1, send_sem, recv_sem)
     two = Halo(2, two_ref, top2, bottom2, left2, right2, send_sem, recv_sem)
     for halo in (zero, one, two):
@@ -339,15 +482,19 @@
         prior = jnp.concatenate([wide[0], nil], axis=0)
         return jnp.concatenate([part.T for part in (upper, lower, after, prior)], axis=0)
 
+    peers = sum(jnp.where(zero.exists(dr, dc), 1, 0) for dr, dc in zero.steps)
+    pl.semaphore_wait(barrier, peers)
+    zero.start(lambda dr, dc: True)
+
+    for copy in loads[0:4]:
+        copy.wait()
     depth = 4 * chan1
     for w_ref, t_ref in ((w1a_ref, t1a), (w1b_ref, t1b)):
         for u in range(3):
             t_ref[u * depth : (u + 1) * depth, :] = blocks(w_ref, u).astype(jnp.bfloat16)
 
-    peers = sum(jnp.where(zero.exists(dr, dc), 1, 0) for dr, dc in zero.steps)
-    pl.semaphore_wait(barrier, peers)
-    zero.start(lambda dr, dc: True)
-
+    for copy in loads[4:8]:
+        copy.wait()
     for u in range(3):
         base = u * depth
         t2a[base : base + chan1, :] = w2a_ref[u, 1]
@@ -469,6 +616,54 @@
             cat_row = jnp.concatenate([down, row[8 : 8 + cols3], up], axis=1)
             cat3b[at(i + k, cols3), :] = cat_row.astype(jnp.bfloat16)
 
+    up = near_ref.shape[1]
+    cols = 2 * pairs
+
+    def put_out(which):
+        return pltpu.make_async_copy(
+            result.at[which], out_ref.at[pl.ds(which * up, up)], out_sem.at[which]
+        )
+
+    def put(row, value, bias):
+        put_row(gather, rows1, row, value, bias)
+
+    def finish(which):
+        take_rows(gather, rows1, result.at[which])
+        put_out(which).start()
+
+    def bias_tile(at_row):
+        return jnp.broadcast_to(bias_ref[at_row : at_row + 1, :], (TILE, up)).T
+
+    def near_lift():
+        loads[8].wait()
+        near = near_ref[...].astype(jnp.float32)
+        near = jnp.concatenate([near, near], axis=0).T.astype(jnp.bfloat16)
+        bias = bias_tile(8)
+        for r in range(rows1):
+            row = one_ref[r].astype(jnp.float32)
+            way = r % 2
+            expand1[way, pl.ds(0, pairs, stride=2), :] = jnp.where(half_own, row, 0.0)
+            expand1[way, pl.ds(1, pairs, stride=2), :] = jnp.where(half_own, 0.0, row)
+            put(r, product(near, expand1[way].astype(jnp.bfloat16)), bias)
+        finish(0)
+
+    def mid_lift():
+        loads[9].wait()
+        expand2[...] = jnp.zeros_like(expand2)
+        bias = bias_tile(9)
+        factor = mid_ref.shape[0]
+        weight = stacked(mid_ref)
+        for i in range(rows2):
+            row = two_ref[i].astype(jnp.float32)
+            way = i % 2
+            for e in range(factor):
+                expand2[way, e, pl.ds(e, cols2, stride=factor), :] = row
+            wide_row = jnp.concatenate([expand2[way, e] for e in range(factor)], axis=1)
+            total = product(weight, wide_row.astype(jnp.bfloat16))
+            for a in range(factor):
+                put(i * factor + a, total[a * up : (a + 1) * up], bias)
+        finish(1)
+
     zero.wait_recv(beside)
 
     def inner_fill(g, carry):
@@ -518,6 +713,7 @@
     for i in range(2, rows2 - 2, 2):
         out_two(i, 2)
     out_two(rows2 - 2, 1)
+    near_lift()
     one.wait_recv(across)
     fill2a(0, cat2e, top1[0], 0)
     fill2a(1, cat2o, top1[1], 1)
@@ -535,6 +731,7 @@
     for r in range(rows2):
         fill3a(r + 3, cat3o if r % 2 == 0 else cat3e, two_ref[r], r % ways)
     mid_three(2, rows3 - 1, True)
+    mid_lift()
     two.wait_recv(across)
     fill3a(0, cat3e, top2[0], 0)
     fill3a(1, cat3o, top2[1], 1)
@@ -547,16 +744,23 @@
     lhs = [cat3b[u * cols3 : (u + rows3) * cols3, :] for u in range(3)]
     total = conv(lhs, t3b, bias3b).astype(jnp.bfloat16)
     three_ref[...] = total.reshape(rows3, cols3, chan3)
+    three_out = pltpu.make_async_copy(three_ref, three_hbm, load_sem.at[0])
+    three_out.start()
+    for which in range(2):
+        put_out(which).wait()
+    three_out.wait()
     for halo in (zero, one, two):
         halo.wait_send()
 
 
-def levels(bev, convs, bias):
+def levels(bev, convs, lifts, bias):
     rows1, pairs, _ = bev.shape
     w1a, w1b, w2a, w2b, w3a, w3b = convs
     chan1, chan2, chan3 = w1a.shape[2], w2b.shape[2], w3b.shape[2]
     rows2, rows3, cols2, cols3 = rows1 // 2, rows1 // 4, pairs, pairs // 2
-    vmem = pl.BlockSpec(memory_space=pltpu.VMEM)
+    near, mid = lifts
+    up, cols = near.shape[1], 2 * pairs
+    operands = (bev, *convs, *lifts, bias)
     mid1, mid3 = pairs + 16, cols3 + 16
 
     def buffers(rows, before, after):
@@ -572,14 +776,20 @@
 
     return pl.pallas_call(
         levels_kernel,
-        in_specs=[vmem] * 8,
-        out_specs=[vmem] * 3,
+        in_specs=[pl.BlockSpec(memory_space=pl.ANY)] * len(operands),
+        out_specs=[pl.BlockSpec(memory_space=pl.ANY)] * 2,
         out_shape=[
-            jax.ShapeDtypeStruct((rows1, pairs, TILE), jnp.bfloat16),
-            jax.ShapeDtypeStruct((rows2, cols2, chan2), jnp.bfloat16),
+            jax.ShapeDtypeStruct((2 * up, rows1, cols), jnp.bfloat16),
             jax.ShapeDtypeStruct((rows3, cols3, chan3), jnp.bfloat16),
         ],
-        scratch_shapes=buffers(rows1, 2, 2)
+        scratch_shapes=[pltpu.VMEM(operand.shape, operand.dtype) for operand in operands]
+        + [
+            pltpu.SemaphoreType.DMA((len(operands),)),
+            half(rows1, pairs, TILE),
+            half(rows2, cols2, chan2),
+            half(rows3, cols3, chan3),
+        ]
+        + buffers(rows1, 2, 2)
         + buffers(rows1, 3, 2)
         + buffers(rows2, 3, 2)
         + [pltpu.SemaphoreType.DMA((3, len(STEPS)))] * 2
@@ -601,119 +811,15 @@
             pltpu.VMEM((4, mid1 + 16, TILE), jnp.float32),
             pltpu.VMEM((4, cols2 + 2 * SIDE + 16, TILE), jnp.float32),
             pltpu.VMEM((4, mid3 + 16, chan3), jnp.float32),
+            half(2, up, rows1, cols),
+            pltpu.VMEM((2, cols, TILE), jnp.float32),
+            pltpu.VMEM((2, mid.shape[0], cols, TILE), jnp.float32),
+            pltpu.VMEM((cols // TILE, up * rows1, TILE), jnp.float32),
+            pltpu.SemaphoreType.DMA((2,)),
         ],
         compiler_params=pltpu.CompilerParams(collective_id=8, has_side_effects=True),
         name="levels",
-    )(bev, *convs, bias)
-
-
-def lift_kernel(
-    one_ref, two_ref, three_ref, near_ref, mid_ref, far_ref, bias_ref, out_ref,
-    result, expand1, expand2, expand3, gather, sem,
-):
-    rows, pairs, _ = one_ref.shape
-    up = near_ref.shape[1]
-    cols = 2 * pairs
-    near = near_ref[...].astype(jnp.float32)
-    near = jnp.concatenate([near, near], axis=0).T.astype(jnp.bfloat16)
-    expand2[...] = jnp.zeros_like(expand2)
-    expand3[...] = jnp.zeros_like(expand3)
-    first_half = lax.broadcasted_iota(jnp.int32, (pairs, TILE), 1) < TILE // 2
-
-    def product(weight, wide):
-        return lax.dot_general(
-            weight, wide, (((1,), (1,)), ((), ())), preferred_element_type=jnp.float32
-        )
-
-    def put(row, value, bias):
-        for h in range(cols // TILE):
-            piece = jnp.maximum(value[:, h * TILE : (h + 1) * TILE] + bias, 0.0)
-            gather[h, pl.ds(row, up, stride=rows), :] = piece
-
-    def finish(which):
-        for h in range(cols // TILE):
-            done = gather[h].astype(jnp.bfloat16).reshape(up, rows, TILE)
-            result[which, :, :, h * TILE : (h + 1) * TILE] = done
-        pltpu.make_async_copy(
-            result.at[which], out_ref.at[pl.ds(which * up, up)], sem.at[which]
-        ).start()
-
-    def bias_tile(at_row):
-        return jnp.broadcast_to(bias_ref[at_row : at_row + 1, :], (TILE, up)).T
-
-    bias = bias_tile(8)
-    for r in range(rows):
-        row = one_ref[r].astype(jnp.float32)
-        way = r % 2
-        expand1[way, pl.ds(0, pairs, stride=2), :] = jnp.where(first_half, row, 0.0)
-        expand1[way, pl.ds(1, pairs, stride=2), :] = jnp.where(first_half, 0.0, row)
-        put(r, product(near, expand1[way].astype(jnp.bfloat16)), bias)
-    finish(0)
-
-    bias = bias_tile(9)
-    factor = mid_ref.shape[0]
-    weight = [
-        jnp.concatenate([mid_ref[a, e] for e in range(factor)], axis=1) for a in range(factor)
-    ]
-    weight = jnp.concatenate(weight, axis=0)
-    for i in range(two_ref.shape[0]):
-        row = two_ref[i].astype(jnp.float32)
-        way = i % 2
-        for e in range(factor):
-            expand2[way, e, pl.ds(e, row.shape[0], stride=factor), :] = row
-        wide = jnp.concatenate([expand2[way, e] for e in range(factor)], axis=1)
-        total = product(weight, wide.astype(jnp.bfloat16))
-        for a in range(factor):
-            put(i * factor + a, total[a * up : (a + 1) * up], bias)
-    finish(1)
-
-    bias = bias_tile(10)
-    factor = far_ref.shape[0]
-    weight = [
-        jnp.concatenate([far_ref[a, e] for e in range(factor)], axis=1) for a in range(factor)
-    ]
-    weight = jnp.concatenate(weight, axis=0)
-    halves = three_ref.shape[2] // TILE
-    for i in range(three_ref.shape[0]):
-        row = three_ref[i].astype(jnp.float32)
-        for e in range(factor):
-            for h in range(halves):
-                expand3[e * halves + h, pl.ds(e, row.shape[0], stride=factor), :] = row[
-                    :, h * TILE : (h + 1) * TILE
-                ]
-        wide = jnp.concatenate([expand3[k] for k in range(factor * halves)], axis=1)
-        total = product(weight, wide.astype(jnp.bfloat16))
-        for a in range(factor):
-            put(i * factor + a, total[a * up : (a + 1) * up], bias)
-    finish(2)
-    for which in range(3):
-        pltpu.make_async_copy(
-            result.at[which], out_ref.at[pl.ds(which * up, up)], sem.at[which]
-        ).wait()
-
-
-def lifts(maps, weights, bias):
-    rows, pairs, _ = maps[0].shape
-    near, mid, far = weights
-    up = near.shape[1]
-    cols = 2 * pairs
-    vmem = pl.BlockSpec(memory_space=pltpu.VMEM)
-    factor, halves = far.shape[0], far.shape[3] // TILE
-    return pl.pallas_call(
-        lift_kernel,
-        in_specs=[vmem] * 7,
-        out_specs=pl.BlockSpec(memory_space=pl.ANY),
-        out_shape=jax.ShapeDtypeStruct((3 * up, rows, cols), jnp.bfloat16),
-        scratch_shapes=[
-            pltpu.VMEM((3, up, rows, cols), jnp.bfloat16),
-            pltpu.VMEM((2, cols, TILE), jnp.float32),
-            pltpu.VMEM((2, mid.shape[0], cols, TILE), jnp.float32),
-            pltpu.VMEM((factor * halves, cols, TILE), jnp.float32),
-            pltpu.VMEM((cols // TILE, up * rows, TILE), jnp.float32),
-            pltpu.SemaphoreType.DMA((3,)),
-        ],
-        name="lifts",
-    )(*maps, near, mid, far, bias)
+    )(*operands)
 
 
 def on_device(
@@ -757,9 +863,9 @@
         fifth_conv,
         sixth_conv,
     )
-    maps = levels(bev, convs, bias)
     near = jnp.transpose(near_lift, (0, 1, 3, 2)).reshape(near_lift.shape[3], near_lift.shape[2])
-    return lifts(maps, (near, mid_lift, far_lift), bias)
+    upper, three = levels(bev, convs, (near, mid_lift), bias)
+    return far_lift_all(upper, three, far_lift, bias)
 
 
 def solution(mesh):

time: 63.1 us -> 59.3 us (0.940)
  Pallas kernels: 62.7 us -> 58.8 us
    pallas_call x3, Pallas kernels: 54.2 us -> 50.3 us  [the longest x1 23 us: levels(): pl.pallas_call(levels_kernel, in_specs=[pl.BlockSpec(memory_space=pl.ANY)...]
where the time goes in v3:
time: 59.3 us; the launch traced here: 59 us
  Pallas kernels  58.8 us (99%)
    pallas_call x1, Pallas kernels, levels(): pl.pallas_call(levels_kernel, in_specs=[pl.BlockSpec(memory_space=pl.ANY)...  23 us
    pallas_call x1, Pallas kernels, encode_all(): pl.pallas_call(encode_kernel, in_specs=[pl.BlockSpec(memory_space=pl.ANY)...  22 us
    pallas_call x1, Pallas kernels, scatter_max(): pl.pallas_call(scatter_kernel, in_specs=[pl.BlockSpec(memory_space=pltpu....  8.47 us
    pallas_call x1, Pallas kernels, far_lift_all(): pl.pallas_call(far_kernel, in_specs=[pl.BlockSpec(memory_space=pl.ANY)] *...  5.32 us

profile of v3, /device:TPU:9, one launch (start us, length us, event | category | flops | bytes accessed | tf_op | source)
XLA Modules:
  0.0 59.0 jit_solution(7346338560763363829)
XLA Ops:
  0.0 22.0 %encode_send.1 = (bf16[16,64,256]{2,1,0:T(8,128)(2,1)}, s32[16,1,256]{2,1,0:T(1,128)}) custom-call(bf16[9,32,4096]{2,1,0:T(8,128)(2,1)} %x_ref.1, s32[16,1,256]{2,1,0:T(1,128)} %bitcast.15, s32[16,1,256]{2,1,0:T(1,128)} %bitcast.16, bf16[9,64]{1,0:T(8,128)(2,1)} %bitcast.19, bf16[64,64]{1,0:T(8,128)(2,1)} %mix_ref.1, f32[11,128]{1,0:T(8,128)} %bitcast.12, ...), custom_call_target="tpu_custom_call" | custom-call | tf_op jit(solution)/shard_map/encode_send/pallas_call | solution.py:153
  22.0 8.5 %scatter_max.1 = bf16[2048,128]{1,0:T(8,128)(2,1)} custom-call(s32[4096]{0:T(1024)} %bitcast.18, bf16[16,64,256]{2,1,0:T(8,128)(2,1)} %get-tuple-element.10.vec_ref), custom_call_target="tpu_custom_call" | custom-call | tf_op jit(solution)/shard_map/scatter_max/pallas_call | solution.py:233
  30.5 23.0 %levels.1 = (bf16[256,16,256]{2,1,0:T(8,128)(2,1)}, bf16[4,64,256]{2,1,0:T(8,128)(2,1)}) custom-call(bf16[16,128,128]{2,1,0:T(8,128)(2,1)} %bitcast.10, bf16[3,3,64,64]{3,2,1,0:T(8,128)(2,1)} %w1a_hbm.1, bf16[3,3,64,64]{3,2,1,0:T(8,128)(2,1)} %w1b_hbm.1, bf16[3,3,64,128]{3,2,1,0:T(8,128)(2,1)} %bitcast.11, bf16[3,3,128,128]{3,2,1,0:T(8,128)(2,1)} %w2b_hbm.1, ...), custom_call_target="tpu_custom_call" | custom-call | tf_op jit(solution)/shard_map/levels/pallas_call | solution.py:777
  53.5 5.3 %far_lift.1 = bf16[384,16,256]{2,1,0:T(8,128)(2,1)} custom-call(bf16[256,16,256]{2,1,0:T(8,128)(2,1)} %get-tuple-element.11.upper_hbm, bf16[4,64,256]{2,1,0:T(8,128)(2,1)} %get-tuple-element.12.three_hbm, bf16[4,4,128,256]{3,2,1,0:T(8,128)(2,1)} %far_hbm.1, f32[11,128]{1,0:T(8,128)} %bitcast.14), custom_call_target="tpu_custom_call" | custom-call | tf_op jit(solution)/shard_map/far_lift/pallas_call | solution.py:410
